TPU v7x, 32 devices: a whole 2x2x4 slice. The times are simulated.
32 devices in a mesh: dp: 8 (over z, x), segment: 4 (over y, core).
Axes of the slice: x: 2, y: 2, z: 4, core: 2. Of those that a mesh axis runs over, the one named last changes fastest.
Arguments:
- latents: float32 [24, 4, 4, 16, 16], P('dp'), may hold values from -6 to 6
- noise_draw: float32 [24, 4, 4, 16, 16], P('dp'), may hold values from -6 to 6
- timesteps: int32 [24], P('dp'), may hold values from 1 to 999
- captions: bfloat16 [24, 300, 4096], P('dp'), may hold values from -2 to 2
- caption_len: int32 [24], P('dp'), may hold values from 1 to 300, as said below
- attention_weights: float32 [12, 384, 384], P(None, None, 'dp'), may hold values from -0.3125 to 0.3125
- feed_weights: float32 [4, 384, 1536], P(None, None, 'dp')
- side_weights: float32 [7456, 384], P(None, 'dp')
- vector_weights: float32 [45, 384], P(None, 'dp'), may hold values from -3 to 3
- attention_momentum: float32 [12, 384, 384], P(None, None, 'dp'), may hold values from -2.670288e-05 to 2.670288e-05
- feed_momentum: float32 [4, 384, 1536], P(None, None, 'dp'), may hold values from -2.670288e-05 to 2.670288e-05
- side_first: float32 [7456, 384], P(None, 'dp'), may hold values from -3.33786e-06 to 3.33786e-06
- side_second: float32 [7456, 384], P(None, 'dp'), may hold values from 3.566765e-15 to 1.426706e-14
- vector_first: float32 [45, 384], P(None, 'dp'), may hold values from -3.0517578e-05 to 3.0517578e-05
- vector_second: float32 [45, 384], P(None, 'dp'), may hold values from 3.5667652e-13 to 1.4267061e-12
- step_count: int32 [1], replicated, may hold values from 2 to 20
Outputs:
- loss_value: float32 [], replicated
- grad_norm: float32 [], replicated
- attention_new: float32 [12, 384, 384], P(None, None, 'dp')
- attention_moment: float32 [12, 384, 384], P(None, None, 'dp')
- feed_new: float32 [4, 384, 1536], P(None, None, 'dp')
- feed_moment: float32 [4, 384, 1536], P(None, None, 'dp')
- side_new: float32 [7456, 384], P(None, 'dp')
- side_first_new: float32 [7456, 384], P(None, 'dp')
- side_second_new: float32 [7456, 384], P(None, 'dp')
- vector_new: float32 [45, 384], P(None, 'dp')
- vector_first_new: float32 [45, 384], P(None, 'dp')
- vector_second_new: float32 [45, 384], P(None, 'dp')
- attention_bf16: bfloat16 [12, 384, 384], P(None, None, 'dp')
- feed_bf16: bfloat16 [4, 384, 1536], P(None, None, 'dp')
- side_bf16: bfloat16 [7456, 384], P(None, 'dp')
- vector_bf16: bfloat16 [45, 384], P(None, 'dp')
Inputs may be any that keep to these rules, and one draw needn't show every extreme that they name: `caption_len`: each clip has 1 to 300 valid caption tokens, the first clip exactly 300.
All inputs are finite; a program needn't handle non-finite values.
Results may differ from a plain program's by a relative error of at most 0.0015.
The roundings to bfloat16 on the way count: a program that leaves them out, or rounds other values in their place, can miss the bound.
Values may be sent and summed in bfloat16 or wider, within the bound.
A program may use at most 256 MiB of HBM per device.

v0:
```python
import math

import jax
import jax.numpy as jnp
from jax import lax
from jax.sharding import PartitionSpec as P

HEADS = 6


highest = lax.Precision.HIGHEST
snr_gamma = 5.0
max_norm = 0.005
momentum_decay = 0.95
muon_rate = 0.05
adam_rate = 0.02
beta_one = 0.9
beta_two = 0.999
weight_decay = 0.01
coef_a = 3.4445
coef_b = -4.775
coef_c = 2.0315


def from_behind(shard, axis, by):
    devices = lax.axis_size(axis)
    pairs = [(i, i + by) for i in range(devices) if 0 <= i + by < devices]
    return lax.ppermute(shard, axis, pairs)


def rounding_pair():

    def round_value(value):
        return lax.optimization_barrier(value.astype(jnp.bfloat16)).astype(jnp.float32)

    def round_front(value):
        return round_value(value)

    def front_keep(value):
        return (round_value(value), None)

    def front_pass(kept, grad):
        return (grad,)

    def round_behind(value):
        return value

    def behind_keep(value):
        return (value, None)

    def behind_low(kept, grad):
        return (round_value(grad),)

    front = jax.custom_vjp(round_front)
    front.defvjp(front_keep, front_pass)
    behind = jax.custom_vjp(round_behind)
    behind.defvjp(behind_keep, behind_low)
    return (front, behind)


def low(value):
    return rounding_pair()[0](value)


def low_back(value):
    return rounding_pair()[1](value)


def matmul(left, right):
    return jnp.dot(left, right, precision=highest, preferred_element_type=jnp.float32)


def two_way(value):
    return low(low_back(value))


def layer_norm(value):
    centred = value - jnp.mean(value, axis=-1, keepdims=True)
    return centred * lax.rsqrt(jnp.mean(centred * centred, axis=-1, keepdims=True) + 1e-06)


def sincos(places, model_width):
    half_width = model_width // 2
    freqs = jnp.exp(-math.log(10000.0) * jnp.arange(half_width, dtype=jnp.float32) / half_width)
    angles = places[:, None] * freqs[None, :]
    return jnp.concatenate([jnp.sin(angles), jnp.cos(angles)], axis=1)


def alpha_level(steps_t):
    return jnp.cos((steps_t.astype(jnp.float32) / 1000.0 + 0.008) / 1.008 * (math.pi / 2)) ** 2


def snr_weight(steps_t):
    level = alpha_level(steps_t)
    ratio = level / (1.0 - level)
    return jnp.minimum(ratio, snr_gamma) / ratio


def patchify(frames):
    count, channels, height, breadth = frames.shape
    grid = frames.reshape(count, channels, height // 2, 2, breadth // 2, 2)
    grid = grid.transpose(0, 2, 4, 3, 5, 1)
    return grid.reshape(count * (height // 2) * (breadth // 2), 4 * channels)


def attend(queries, key_rows, value_rows, allowed):
    score_scale = queries.shape[-1] ** (-0.5)
    scores = low_back(
        jnp.einsum("bqhd,bkhd->bhqk", queries, key_rows, precision=highest) * score_scale
    )
    if allowed is not None:
        scores = jnp.where(allowed, scores, -1e30)
    softmax_out = low(jax.nn.softmax(scores, axis=-1))
    return two_way(jnp.einsum("bhqk,bkhd->bqhd", softmax_out, value_rows, precision=highest))


def time_embed(params, steps_t):
    side_rows, vectors = (params[2], params[3])
    model_width = side_rows.shape[1]
    freqs = jnp.exp(-math.log(10000.0) * jnp.arange(128, dtype=jnp.float32) / 128)
    angles = steps_t.astype(jnp.float32) * freqs
    feature = jnp.concatenate([jnp.cos(angles), jnp.sin(angles)])[None, :]
    hidden = matmul(low(feature), side_rows[16:272]) + vectors[1]
    embedded = matmul(low(jax.nn.silu(hidden)), side_rows[272 : 272 + model_width]) + vectors[2]
    offset = side_rows.shape[0] - 6 * model_width
    modulate = matmul(low(jax.nn.silu(embedded)), side_rows[offset:].T) + vectors[3:9].reshape(-1)
    return (embedded[0], modulate[0].reshape(6, model_width))


def self_attention(resident, modulate, matrices, biases, temporal, frames):
    token_count, model_width = resident.shape

    def split_heads(value):
        value = value.reshape(frames, token_count // frames, HEADS, model_width // HEADS)
        return jnp.swapaxes(value, 0, 1) if temporal else value

    normed = low(layer_norm(resident) * (1.0 + modulate[1]) + modulate[0])
    queries = two_way(matmul(normed, matrices[0]) + biases[0])
    key_rows = two_way(matmul(normed, matrices[1]))
    value_rows = two_way(matmul(normed, matrices[2]) + biases[1])
    mixture = attend(split_heads(queries), split_heads(key_rows), split_heads(value_rows), None)
    if temporal:
        mixture = jnp.swapaxes(mixture, 0, 1)
    branch = low_back(matmul(mixture.reshape(token_count, model_width), matrices[3]) + biases[2])
    return resident + modulate[2] * branch


def cross_attend(resident, matrices, biases, caption_keys, allowed):
    token_count, model_width = resident.shape
    queries = two_way(matmul(low(resident), matrices[0]) + biases[0])
    key_rows = two_way(matmul(caption_keys, matrices[1]))
    value_rows = two_way(matmul(caption_keys, matrices[2]) + biases[1])

    def split_heads(value):
        return value.reshape(1, value.shape[0], HEADS, model_width // HEADS)

    mixture = attend(split_heads(queries), split_heads(key_rows), split_heads(value_rows), allowed)
    return resident + low_back(
        matmul(mixture.reshape(token_count, model_width), matrices[3]) + biases[2]
    )


def feed_forward(resident, modulate, up_proj, down_proj, biases):
    normed = low(layer_norm(resident) * (1.0 + modulate[4]) + modulate[3])
    inner = low_back(matmul(normed, up_proj) + biases[3:7].reshape(-1))
    branch = low_back(matmul(low(jax.nn.gelu(inner, approximate=True)), down_proj.T) + biases[7])
    return resident + modulate[5] * branch


def caption_features(params, caption):
    side_rows, vectors = (params[2], params[3])
    model_width = side_rows.shape[1]
    offset = 272 + model_width
    text_width = caption.shape[1]
    hidden = matmul(low(caption), side_rows[offset : offset + text_width]) + vectors[9]
    second = side_rows[offset + text_width : offset + text_width + model_width]
    return two_way(matmul(low(jax.nn.gelu(hidden, approximate=True)), second) + vectors[10])


def segment_embed(params, resident, sample):
    side_rows, vectors = (params[2], params[3])
    latent, noise_part, steps_t = (sample[0], sample[1], sample[2])
    level = alpha_level(steps_t)
    tokens = jnp.sqrt(level) * patchify(latent) + jnp.sqrt(1.0 - level) * patchify(noise_part)
    count, height = (latent.shape[0], latent.shape[2] // 2)
    model_width = side_rows.shape[1]
    places = jnp.arange(height * height)
    grid_rows = (places // height).astype(jnp.float32)
    grid_cols = (places % height).astype(jnp.float32)
    spatial = jnp.concatenate(
        [sincos(grid_rows, model_width // 2), sincos(grid_cols, model_width // 2)], axis=1
    )
    embedded = matmul(low(tokens), side_rows[0:16]) + vectors[0] + jnp.tile(spatial, (count, 1))
    return (embedded, jnp.zeros((), jnp.float32))


def segment_spatial(params, resident, sample):
    matrices, feeds, vectors = (params[0], params[1], params[3])
    embedded, modulate = time_embed(params, sample[2])
    modulate = vectors[19:25] + modulate
    resident = self_attention(
        resident, modulate, matrices[0:4], vectors[11:14], False, sample[0].shape[0]
    )
    resident = feed_forward(resident, modulate, feeds[0], feeds[1], vectors[11:19])
    return (resident, jnp.zeros((), jnp.float32))


def segment_temporal(params, resident, sample):
    matrices, feeds, vectors = (params[0], params[1], params[3])
    frames = sample[0].shape[0]
    token_count, model_width = resident.shape
    timing = sincos(jnp.arange(frames).astype(jnp.float32), model_width)
    resident = resident + jnp.repeat(timing, token_count // frames, axis=0)
    embedded, modulate = time_embed(params, sample[2])
    modulate = vectors[33:39] + modulate
    resident = self_attention(resident, modulate, matrices[4:8], vectors[25:28], True, frames)
    caption_keys = caption_features(params, sample[3])
    allowed = (jnp.arange(sample[3].shape[0]) < sample[4])[None, None, None, :]
    resident = cross_attend(resident, matrices[8:12], vectors[39:42], caption_keys, allowed)
    resident = feed_forward(resident, modulate, feeds[2], feeds[3], vectors[25:33])
    return (resident, jnp.zeros((), jnp.float32))


def segment_final(params, resident, sample):
    side_rows, vectors = (params[2], params[3])
    model_width = side_rows.shape[1]
    embedded, modulate = time_embed(params, sample[2])
    table = vectors[42:44] + embedded
    normed = low(layer_norm(resident) * (1.0 + table[1]) + table[0])
    offset = side_rows.shape[0] - 6 * model_width - 16
    predicted = low_back(matmul(normed, side_rows[offset : offset + 16].T) + vectors[44, :16])
    target = patchify(sample[1])
    squared = jnp.mean((predicted - target) ** 2)
    return (jnp.zeros_like(resident), snr_weight(sample[2]) * squared)


def pulled(segment_fn):

    def run_back(params, resident, sample, cotangent, error_cot):
        _, pullback = jax.vjp(
            lambda weights, value: segment_fn(weights, value, sample), params, resident
        )
        grads, resident_cot = pullback((cotangent, error_cot))
        return (resident_cot, grads)

    return run_back


def gram_of(matrix):
    return jnp.einsum("mik,mjk->mij", matrix, matrix, precision=highest)


def newton_step(matrix, gram):
    poly = coef_b * gram + coef_c * jnp.einsum("mij,mjk->mik", gram, gram, precision=highest)
    return coef_a * matrix + jnp.einsum("mij,mjk->mik", poly, matrix, precision=highest)


def adamw_update(weight, first, second, grad, count):
    first = beta_one * first + (1.0 - beta_one) * grad
    second = beta_two * second + (1.0 - beta_two) * grad * grad
    first_hat = first / (1.0 - jnp.power(beta_one, count))
    second_hat = second / (1.0 - jnp.power(beta_two, count))
    weight = weight - adam_rate * (
        first_hat / (jnp.sqrt(second_hat) + 1e-08) + weight_decay * weight
    )
    return (weight, first, second)


def body(
    latents,
    noise_draw,
    timesteps,
    captions,
    caption_len,
    attention_weights,
    feed_weights,
    side_weights,
    vector_weights,
    attention_momentum,
    feed_momentum,
    side_first,
    side_second,
    vector_first,
    vector_second,
    step_count,
):
    rank = lax.axis_index("segment")
    segments = lax.axis_size("segment")
    copies = (
        lax.all_gather(attention_weights.astype(jnp.bfloat16), "dp", axis=2, tiled=True),
        lax.all_gather(feed_weights.astype(jnp.bfloat16), "dp", axis=2, tiled=True),
        lax.all_gather(side_weights.astype(jnp.bfloat16), "dp", axis=1, tiled=True),
        lax.all_gather(vector_weights.astype(jnp.bfloat16), "dp", axis=1, tiled=True),
    )
    params = tuple((piece.astype(jnp.float32) for piece in copies))
    total_weight = lax.psum(jnp.sum(snr_weight(timesteps)), "dp")
    micro = latents.shape[0]
    token_count = latents.shape[1] * (latents.shape[3] // 2) * (latents.shape[4] // 2)
    model_width = params[2].shape[1]
    segment_list = [segment_embed, segment_spatial, segment_temporal, segment_final]
    pull_list = [pulled(segment_fn) for segment_fn in segment_list]

    def pick(index):
        chosen = jnp.clip(index, 0, micro - 1)
        return (
            chosen,
            (
                latents[chosen],
                noise_draw[chosen],
                timesteps[chosen],
                captions[chosen].astype(jnp.float32),
                caption_len[chosen],
            ),
        )

    def forward_step(moment, carry):
        incoming, kept, error_sum = carry
        index = moment - rank
        valid = jnp.logical_and(index >= 0, index < micro)
        chosen, sample = pick(index)
        outgoing, error_term = lax.switch(
            rank, segment_list, params, incoming.astype(jnp.float32), sample
        )
        kept = jnp.where(valid, lax.dynamic_update_index_in_dim(kept, incoming, chosen, 0), kept)
        error_sum = error_sum + jnp.where(valid, error_term, 0.0)
        incoming = from_behind(outgoing.astype(jnp.bfloat16), "segment", 1)
        return (incoming, kept, error_sum)

    start_input = jnp.zeros((token_count, model_width), jnp.bfloat16)
    start_kept = jnp.zeros((micro, token_count, model_width), jnp.bfloat16)
    _, kept, error_sum = lax.fori_loop(
        0, micro + segments - 1, forward_step, (start_input, start_kept, jnp.zeros((), jnp.float32))
    )
    local_loss = error_sum / total_weight
    loss_value = lax.psum(local_loss, ("dp", "segment"))

    def backward_step(moment, carry):
        incoming, grads = carry
        index = moment - (segments - 1 - rank)
        valid = jnp.logical_and(index >= 0, index < micro)
        chosen, sample = pick(index)
        resident = lax.dynamic_index_in_dim(kept, chosen, 0, keepdims=False).astype(jnp.float32)
        resident_cot, fresh = lax.switch(
            rank,
            pull_list,
            params,
            resident,
            sample,
            incoming.astype(jnp.float32),
            1.0 / total_weight,
        )
        grads = jax.tree.map(lambda total, term: total + jnp.where(valid, term, 0.0), grads, fresh)
        incoming = from_behind(resident_cot.astype(jnp.bfloat16), "segment", -1)
        return (incoming, grads)

    zero_grads = tuple((jnp.zeros_like(piece) for piece in params))
    _, grads = lax.fori_loop(0, micro + segments - 1, backward_step, (start_input, zero_grads))
    shards = (
        lax.psum_scatter(grads[0], "dp", scatter_dimension=2, tiled=True),
        lax.psum_scatter(grads[1], "dp", scatter_dimension=2, tiled=True),
        lax.psum_scatter(grads[2], "dp", scatter_dimension=1, tiled=True),
        lax.psum_scatter(grads[3], "dp", scatter_dimension=1, tiled=True),
    )
    shards = lax.psum(shards, "segment")
    squares = sum((jnp.sum(piece * piece) for piece in shards))
    norm_sq = lax.psum(squares, "dp")
    grad_norm = jnp.sqrt(norm_sq)
    factor = jnp.minimum(1.0, max_norm / (grad_norm + 1e-06))
    attention_grad, feed_grad, side_grad, vector_grad = (piece * factor for piece in shards)
    attention_moment = momentum_decay * attention_momentum + attention_grad
    feed_moment = momentum_decay * feed_momentum + feed_grad
    attention_look = attention_grad + momentum_decay * attention_moment
    feed_look = feed_grad + momentum_decay * feed_moment
    attention_share = attention_look.shape[0] // segments
    feed_share = feed_look.shape[0] // segments
    own_attention = lax.dynamic_slice_in_dim(
        attention_look, rank * attention_share, attention_share, 0
    )
    own_feed = lax.dynamic_slice_in_dim(feed_look, rank * feed_share, feed_share, 0)
    raw_grams = lax.psum((gram_of(own_attention), gram_of(own_feed)), "dp")
    attention_scale = jnp.sqrt(jnp.trace(raw_grams[0], axis1=1, axis2=2)) + 1e-07
    feed_scale = jnp.sqrt(jnp.trace(raw_grams[1], axis1=1, axis2=2)) + 1e-07
    own_attention = own_attention / attention_scale[:, None, None]
    own_feed = own_feed / feed_scale[:, None, None]
    own_attention = newton_step(
        own_attention, raw_grams[0] / (attention_scale * attention_scale)[:, None, None]
    )
    own_feed = newton_step(own_feed, raw_grams[1] / (feed_scale * feed_scale)[:, None, None])
    for sweep in range(1, 5):
        gram_pair = lax.psum((gram_of(own_attention), gram_of(own_feed)), "dp")
        own_attention = newton_step(own_attention, gram_pair[0])
        own_feed = newton_step(own_feed, gram_pair[1])
    full_attention, full_feed = (
        lax.all_gather(own_attention, "segment", axis=0, tiled=True),
        lax.all_gather(own_feed, "segment", axis=0, tiled=True),
    )
    attention_rate = muon_rate * 0.2 * math.sqrt(params[0].shape[2])
    feed_rate = muon_rate * 0.2 * math.sqrt(params[1].shape[2])
    attention_new = (
        attention_weights * (1.0 - muon_rate * weight_decay) - attention_rate * full_attention
    )
    feed_new = feed_weights * (1.0 - muon_rate * weight_decay) - feed_rate * full_feed
    count = step_count[0].astype(jnp.float32)
    side_new, side_first_new, side_second_new = adamw_update(
        side_weights, side_first, side_second, side_grad, count
    )
    vector_new, vector_first_new, vector_second_new = adamw_update(
        vector_weights, vector_first, vector_second, vector_grad, count
    )
    return (
        loss_value,
        grad_norm,
        attention_new,
        attention_moment,
        feed_new,
        feed_moment,
        side_new,
        side_first_new,
        side_second_new,
        vector_new,
        vector_first_new,
        vector_second_new,
        attention_new.astype(jnp.bfloat16),
        feed_new.astype(jnp.bfloat16),
        side_new.astype(jnp.bfloat16),
        vector_new.astype(jnp.bfloat16),
    )


def solution(mesh):
    return jax.shard_map(
        body,
        mesh=mesh,
        in_specs=(
            P("dp", None, None, None, None),
            P("dp", None, None, None, None),
            P("dp"),
            P("dp", None, None),
            P("dp"),
            P(None, None, "dp"),
            P(None, None, "dp"),
            P(None, "dp"),
            P(None, "dp"),
            P(None, None, "dp"),
            P(None, None, "dp"),
            P(None, "dp"),
            P(None, "dp"),
            P(None, "dp"),
            P(None, "dp"),
            P(),
        ),
        out_specs=(
            P(),
            P(),
            P(None, None, "dp"),
            P(None, None, "dp"),
            P(None, None, "dp"),
            P(None, None, "dp"),
            P(None, "dp"),
            P(None, "dp"),
            P(None, "dp"),
            P(None, "dp"),
            P(None, "dp"),
            P(None, "dp"),
            P(None, None, "dp"),
            P(None, None, "dp"),
            P(None, "dp"),
            P(None, "dp"),
        ),
        check_vma=False,
    )
```

profile of v0, /device:TPU:27, one launch (start us, length us, event | category | flops | bytes accessed | tf_op | source)
XLA Modules:
  0.0 3107.3 jit_solution(13586465682064179020)
XLA Ops:
  82.5 74.6 %all-gather.9.cloned.1.call-done = bf16[4,384,1536]{1,0,2:T(4,128)(2,1)} async-done(((bf16[4,384,192]{1,0,2:T(4,128)(2,1)}), bf16[4,384,1536]{1,0,2:T(4,128)(2,1)}) %all-gather.9.cloned.1.call-update) | async-done | bytes 4718608 | tf_op jit(solution)/shard_map/all_gather | solution.py:291
  166.7 84.4 %all-gather.5.cloned.1.call-done = bf16[7456,384]{0,1:T(8,128)(2,1)} async-done(((bf16[7456,48]{0,1:T(8,128)(2,1)}), bf16[7456,384]{0,1:T(8,128)(2,1)}) %all-gather.5.cloned.1.call-update) | async-done | bytes 5726224 | tf_op jit(solution)/shard_map/all_gather | solution.py:292
  261.0 373.9 %while.42 = (s32[]{:T(128)}, bf16[256,384]{1,0:T(8,128)(2,1)S(1)}, bf16[3,256,384]{2,1,0:T(8,128)(2,1)}, f32[]{:T(128)}, s32[]{:T(128)}, /*index=5*/s32[3]{0:T(1...) while((s32[]{:T(128)}, bf16[256,384]{1,0:T(8,128)(2,1)S(1)}, ...), condition=%wide.region_22.23_spmd, body=%wide.region_0.22_spmd.sunk | while | flops 13741672448 | bytes 54284988 | solution.py:331
  368.2 29.3 collective-permute-start
  426.9 29.3 collective-permute-start
  485.6 29.3 collective-permute-start
  544.3 29.3 collective-permute-start
  603.0 29.3 collective-permute-start
  634.9 1132.9 %while.43 = (s32[]{:T(128)}, bf16[256,384]{1,0:T(8,128)(2,1)S(1)}, f32[12,384,384]{2,1,0:T(8,128)}, f32[4,384,1536]{2,1,0:T(8,128)}, f32[7456,384]{1,0:T(8,128)}...) while((s32[]{:T(128)}, bf16[256,384]{1,0:T(8,128)(2,1)S(1)}, ...), condition=%wide.region_92.93_spmd.clone, body=%wide.region_26.92_spmd.clone.sunk | while | flops 29575989248 | bytes 372953248 | solution.py:357
  643.6 100.5 %conditional.6 = (bf16[256,384]{1,0:T(8,128)(2,1)}, f32[12,384,384]{2,1,0:T(8,128)}, f32[4,384,1536]{2,1,0:T(8,128)}, f32[7456,384]{1,0:T(8,128)}, f32[45,384]{1,0:T(8,128)}) conditional(s32[]{:T(128)} %get-tuple-element.1800, (s32[]{:T(128)}, f32[3,4,4,16,16]{2,4,3,1,0:T(8,128)}, s32[]{:T(128)}, ...), branch_computations={%region_27.28_spmd, %region_29.51_spmd, %region_52.82_spmd, %regio... | conditional | flops 29554765824 | bytes 285737888 | solution.py:343
  760.7 47.3 %collective-permute-done.1 = bf16[256,384]{1,0:T(8,128)(2,1)S(1)} collective-permute-done((bf16[256,384]{1,0:T(8,128)(2,1)}, bf16[256,384]{1,0:T(8,128)(2,1)S(1)}, u32[]{:S(2)}, u32[]{:S(2)}) %collective-permute-start.1) | collective-permute-done | bytes 196640 | tf_op jit(solution)/shard_map/while/body/eval_jaxpr/ppermute | solution.py:28
  810.9 100.6 %conditional.6 = (bf16[256,384]{1,0:T(8,128)(2,1)}, f32[12,384,384]{2,1,0:T(8,128)}, f32[4,384,1536]{2,1,0:T(8,128)}, f32[7456,384]{1,0:T(8,128)}, f32[45,384]{1,0:T(8,128)}) conditional(s32[]{:T(128)} %get-tuple-element.1800, (s32[]{:T(128)}, f32[3,4,4,16,16]{2,4,3,1,0:T(8,128)}, s32[]{:T(128)}, ...), branch_computations={%region_27.28_spmd, %region_29.51_spmd, %region_52.82_spmd, %regio... | conditional | flops 29554765824 | bytes 285737888 | solution.py:343
  939.7 44.6 %collective-permute-done.1 = bf16[256,384]{1,0:T(8,128)(2,1)S(1)} collective-permute-done((bf16[256,384]{1,0:T(8,128)(2,1)}, bf16[256,384]{1,0:T(8,128)(2,1)S(1)}, u32[]{:S(2)}, u32[]{:S(2)}) %collective-permute-start.1) | collective-permute-done | bytes 196640 | tf_op jit(solution)/shard_map/while/body/eval_jaxpr/ppermute | solution.py:28
  987.3 100.6 %conditional.6 = (bf16[256,384]{1,0:T(8,128)(2,1)}, f32[12,384,384]{2,1,0:T(8,128)}, f32[4,384,1536]{2,1,0:T(8,128)}, f32[7456,384]{1,0:T(8,128)}, f32[45,384]{1,0:T(8,128)}) conditional(s32[]{:T(128)} %get-tuple-element.1800, (s32[]{:T(128)}, f32[3,4,4,16,16]{2,4,3,1,0:T(8,128)}, s32[]{:T(128)}, ...), branch_computations={%region_27.28_spmd, %region_29.51_spmd, %region_52.82_spmd, %regio... | conditional | flops 29554765824 | bytes 285737888 | solution.py:343
  1125.0 56.3 %collective-permute-done.1 = bf16[256,384]{1,0:T(8,128)(2,1)S(1)} collective-permute-done((bf16[256,384]{1,0:T(8,128)(2,1)}, bf16[256,384]{1,0:T(8,128)(2,1)S(1)}, u32[]{:S(2)}, u32[]{:S(2)}) %collective-permute-start.1) | collective-permute-done | bytes 196640 | tf_op jit(solution)/shard_map/while/body/eval_jaxpr/ppermute | solution.py:28
  1184.3 100.6 %conditional.6 = (bf16[256,384]{1,0:T(8,128)(2,1)}, f32[12,384,384]{2,1,0:T(8,128)}, f32[4,384,1536]{2,1,0:T(8,128)}, f32[7456,384]{1,0:T(8,128)}, f32[45,384]{1,0:T(8,128)}) conditional(s32[]{:T(128)} %get-tuple-element.1800, (s32[]{:T(128)}, f32[3,4,4,16,16]{2,4,3,1,0:T(8,128)}, s32[]{:T(128)}, ...), branch_computations={%region_27.28_spmd, %region_29.51_spmd, %region_52.82_spmd, %regio... | conditional | flops 29554765824 | bytes 285737888 | solution.py:343
  1322.0 56.3 %collective-permute-done.1 = bf16[256,384]{1,0:T(8,128)(2,1)S(1)} collective-permute-done((bf16[256,384]{1,0:T(8,128)(2,1)}, bf16[256,384]{1,0:T(8,128)(2,1)S(1)}, u32[]{:S(2)}, u32[]{:S(2)}) %collective-permute-start.1) | collective-permute-done | bytes 196640 | tf_op jit(solution)/shard_map/while/body/eval_jaxpr/ppermute | solution.py:28
  1381.2 100.6 %conditional.6 = (bf16[256,384]{1,0:T(8,128)(2,1)}, f32[12,384,384]{2,1,0:T(8,128)}, f32[4,384,1536]{2,1,0:T(8,128)}, f32[7456,384]{1,0:T(8,128)}, f32[45,384]{1,0:T(8,128)}) conditional(s32[]{:T(128)} %get-tuple-element.1800, (s32[]{:T(128)}, f32[3,4,4,16,16]{2,4,3,1,0:T(8,128)}, s32[]{:T(128)}, ...), branch_computations={%region_27.28_spmd, %region_29.51_spmd, %region_52.82_spmd, %regio... | conditional | flops 29554765824 | bytes 285737888 | solution.py:343
  1518.9 56.3 %collective-permute-done.1 = bf16[256,384]{1,0:T(8,128)(2,1)S(1)} collective-permute-done((bf16[256,384]{1,0:T(8,128)(2,1)}, bf16[256,384]{1,0:T(8,128)(2,1)S(1)}, u32[]{:S(2)}, u32[]{:S(2)}) %collective-permute-start.1) | collective-permute-done | bytes 196640 | tf_op jit(solution)/shard_map/while/body/eval_jaxpr/ppermute | solution.py:28
  1578.2 100.6 %conditional.6 = (bf16[256,384]{1,0:T(8,128)(2,1)}, f32[12,384,384]{2,1,0:T(8,128)}, f32[4,384,1536]{2,1,0:T(8,128)}, f32[7456,384]{1,0:T(8,128)}, f32[45,384]{1,0:T(8,128)}) conditional(s32[]{:T(128)} %get-tuple-element.1800, (s32[]{:T(128)}, f32[3,4,4,16,16]{2,4,3,1,0:T(8,128)}, s32[]{:T(128)}, ...), branch_computations={%region_27.28_spmd, %region_29.51_spmd, %region_52.82_spmd, %regio... | conditional | flops 29554765824 | bytes 285737888 | solution.py:343
  1707.0 56.3 %collective-permute-done.1 = bf16[256,384]{1,0:T(8,128)(2,1)S(1)} collective-permute-done((bf16[256,384]{1,0:T(8,128)(2,1)}, bf16[256,384]{1,0:T(8,128)(2,1)S(1)}, u32[]{:S(2)}, u32[]{:S(2)}) %collective-permute-start.1) | collective-permute-done | bytes 196640 | tf_op jit(solution)/shard_map/while/body/eval_jaxpr/ppermute | solution.py:28
  1799.7 126.4 %reduce-scatter.7.cloned.1.call-done = f32[12,384,48]{1,2,0:T(8,128)} async-done(((f32[12,384,384]{1,2,0:T(8,128)}), f32[12,384,48]{1,2,0:T(8,128)}) %reduce-scatter.7.cloned.1.call-update) | async-done | bytes 884752 | tf_op jit(solution)/shard_map/reduce_scatter | solution.py:359
  1926.1 166.2 %reduce-scatter.9.cloned.1.call-done = f32[4,384,192]{1,2,0:T(8,128)} async-done(((f32[4,384,1536]{1,2,0:T(8,128)}), f32[4,384,192]{1,2,0:T(8,128)}) %reduce-scatter.9.cloned.1.call-update) | async-done | bytes 1179664 | tf_op jit(solution)/shard_map/reduce_scatter | solution.py:360
  2092.4 197.1 %reduce-scatter.11.cloned.1.call-done = f32[7456,48]{0,1:T(8,128)} async-done(((f32[7456,384]{0,1:T(8,128)}), f32[7456,48]{0,1:T(8,128)}) %reduce-scatter.11.cloned.1.call-update) | async-done | bytes 1431568 | tf_op jit(solution)/shard_map/reduce_scatter | solution.py:361
  2289.6 62.1 %reduce-scatter.13.cloned.1.call-done = f32[48,45]{1,0:T(8,128)} async-done(((f32[384,45]{1,0:T(8,128)}), f32[48,45]{1,0:T(8,128)}) %reduce-scatter.13.cloned.1.call-update) | async-done | bytes 8656
  2365.2 66.8 %all-reduce.101.cloned.1.call-done = (f32[12,384,48]{1,2,0:T(8,128)}, f32[4,384,192]{1,2,0:T(8,128)}, f32[7456,48]{0,1:T(8,128)}) async-done(((f32[12,384,48]{1,2,0:T(8,128)}, f32[4,384,192]{1,2,0:T(8,128)}, f32[7456,48]{0,1:T(8,128)}), (f32[12,384,48]{1,2,0:T(8,128)}, f32[4,384,192]{1,2,0:T(8,128)}, f32[7456,48]{0,1:T(8,128)})) %all-reduce.101.cloned.1.call-update) | async-done | bytes 3495952 | tf_op jit(solution)/shard_map/psum | solution.py:364
  2462.7 111.2 %all-reduce.99.cloned.1.call-done = (f32[3,384,384]{2,1,0:T(8,128)}, f32[1,384,384]{2,1,0:T(8,128)}) async-done(((f32[3,384,384]{2,1,0:T(8,128)}, f32[1,384,384]{2,1,0:T(8,128)}), (f32[3,384,384]{2,1,0:T(8,128)}, f32[1,384,384]{2,1,0:T(8,128)})) %all-reduce.99.cloned.1.call-update) | async-done | bytes 2359312 | tf_op jit(solution)/shard_map/psum | solution.py:380
  2590.5 108.0 %all-reduce.97.cloned.1.call-done = (f32[3,384,384]{2,1,0:T(8,128)}, f32[1,384,384]{2,1,0:T(8,128)}) async-done(((f32[3,384,384]{2,1,0:T(8,128)}, f32[1,384,384]{2,1,0:T(8,128)}), (f32[3,384,384]{2,1,0:T(8,128)}, f32[1,384,384]{2,1,0:T(8,128)})) %all-reduce.97.cloned.1.call-update) | async-done | bytes 2359312 | tf_op jit(solution)/shard_map/psum | solution.py:390
  2713.3 108.0 %all-reduce.95.cloned.1.call-done = (f32[3,384,384]{2,1,0:T(8,128)}, f32[1,384,384]{2,1,0:T(8,128)}) async-done(((f32[3,384,384]{2,1,0:T(8,128)}, f32[1,384,384]{2,1,0:T(8,128)}), (f32[3,384,384]{2,1,0:T(8,128)}, f32[1,384,384]{2,1,0:T(8,128)})) %all-reduce.95.cloned.1.call-update) | async-done | bytes 2359312 | tf_op jit(solution)/shard_map/psum | solution.py:390
  2836.4 107.8 %all-reduce.93.cloned.1.call-done = (f32[3,384,384]{2,1,0:T(8,128)}, f32[1,384,384]{2,1,0:T(8,128)}) async-done(((f32[3,384,384]{2,1,0:T(8,128)}, f32[1,384,384]{2,1,0:T(8,128)}), (f32[3,384,384]{2,1,0:T(8,128)}, f32[1,384,384]{2,1,0:T(8,128)})) %all-reduce.93.cloned.1.call-update) | async-done | bytes 2359312 | tf_op jit(solution)/shard_map/psum | solution.py:390
  2960.3 41.9 %psum.120 = f32[]{:T(128)} all-reduce(f32[]{:T(128)S(6)} %div.461), channel_id=1, replica_groups=mesh['dp'=8,'segment'=4] {'dp','segment'}, use_global_device_ids=true, to_apply=%region_25.26 | all-reduce | flops 1 | bytes 8 | tf_op jit(solution)/shard_map/psum | solution.py:335
  3002.2 66.0 %all-reduce.91.cloned.1.call-done = (f32[3,384,384]{2,1,0:T(8,128)}, f32[1,384,384]{2,1,0:T(8,128)}) async-done(((f32[3,384,384]{2,1,0:T(8,128)}, f32[1,384,384]{2,1,0:T(8,128)}), (f32[3,384,384]{2,1,0:T(8,128)}, f32[1,384,384]{2,1,0:T(8,128)})) %all-reduce.91.cloned.1.call-update) | async-done | bytes 2359312 | tf_op jit(solution)/shard_map/psum | solution.py:390
  (1759 shorter events, 1319.3 us)
Async XLA Ops:
  7.2 68.9 %all-gather.7.cloned.1.call-start = ((), (), s32[]{:S(2)}) async-start(), calls=%async_computation.5 | async-start | bytes 3981312 | tf_op jit(solution)/shard_map/all_gather | solution.py:290
  9.4 147.7 %all-gather.9.cloned.1.call-start = ((), (), s32[]{:S(2)}) async-start(), calls=%async_computation.6 | async-start | bytes 5308416 | tf_op jit(solution)/shard_map/all_gather | solution.py:291
  11.1 240.1 %all-gather.5.cloned.1.call-start = ((), (), s32[]{:S(2)}) async-start(), calls=%async_computation.4 | async-start | bytes 6524928 | tf_op jit(solution)/shard_map/all_gather | solution.py:292
  12.1 1914.0 %reduce-scatter.7.cloned.1.call-start = ((), (), s32[]{:S(2)}) async-start(), calls=%async_computation.7 | async-start | bytes 7962624 | tf_op jit(solution)/shard_map/reduce_scatter | solution.py:359
  310.4 30.9 collective-permute-start
  368.2 31.9 %collective-permute-start = (bf16[256,384]{1,0:T(8,128)(2,1)S(1)}, bf16[256,384]{1,0:T(8,128)(2,1)S(1)}, u32[]{:S(2)}, u32[]{:S(2)}) collective-permute-start(bf16[256,384]{1,0:T(8,128)(2,1)S(1)} %get-tuple-element.1622), channel_id=1, source_target_pairs={{0,1},{1,2},{2,3},{4,5},{5,6},{6,7},{8,9},{9,10},{10,11},{12,13},{... | collective-permute-start | bytes 589832 | tf_op jit(solution)/shard_map/while/body/eval_jaxpr/ppermute | solution.py:28
  426.9 31.9 %collective-permute-start = (bf16[256,384]{1,0:T(8,128)(2,1)S(1)}, bf16[256,384]{1,0:T(8,128)(2,1)S(1)}, u32[]{:S(2)}, u32[]{:S(2)}) collective-permute-start(bf16[256,384]{1,0:T(8,128)(2,1)S(1)} %get-tuple-element.1622), channel_id=1, source_target_pairs={{0,1},{1,2},{2,3},{4,5},{5,6},{6,7},{8,9},{9,10},{10,11},{12,13},{... | collective-permute-start | bytes 589832 | tf_op jit(solution)/shard_map/while/body/eval_jaxpr/ppermute | solution.py:28
  485.6 31.9 %collective-permute-start = (bf16[256,384]{1,0:T(8,128)(2,1)S(1)}, bf16[256,384]{1,0:T(8,128)(2,1)S(1)}, u32[]{:S(2)}, u32[]{:S(2)}) collective-permute-start(bf16[256,384]{1,0:T(8,128)(2,1)S(1)} %get-tuple-element.1622), channel_id=1, source_target_pairs={{0,1},{1,2},{2,3},{4,5},{5,6},{6,7},{8,9},{9,10},{10,11},{12,13},{... | collective-permute-start | bytes 589832 | tf_op jit(solution)/shard_map/while/body/eval_jaxpr/ppermute | solution.py:28
  544.3 31.9 %collective-permute-start = (bf16[256,384]{1,0:T(8,128)(2,1)S(1)}, bf16[256,384]{1,0:T(8,128)(2,1)S(1)}, u32[]{:S(2)}, u32[]{:S(2)}) collective-permute-start(bf16[256,384]{1,0:T(8,128)(2,1)S(1)} %get-tuple-element.1622), channel_id=1, source_target_pairs={{0,1},{1,2},{2,3},{4,5},{5,6},{6,7},{8,9},{9,10},{10,11},{12,13},{... | collective-permute-start | bytes 589832 | tf_op jit(solution)/shard_map/while/body/eval_jaxpr/ppermute | solution.py:28
  603.0 31.9 %collective-permute-start = (bf16[256,384]{1,0:T(8,128)(2,1)S(1)}, bf16[256,384]{1,0:T(8,128)(2,1)S(1)}, u32[]{:S(2)}, u32[]{:S(2)}) collective-permute-start(bf16[256,384]{1,0:T(8,128)(2,1)S(1)} %get-tuple-element.1622), channel_id=1, source_target_pairs={{0,1},{1,2},{2,3},{4,5},{5,6},{6,7},{8,9},{9,10},{10,11},{12,13},{... | collective-permute-start | bytes 589832 | tf_op jit(solution)/shard_map/while/body/eval_jaxpr/ppermute | solution.py:28
  744.1 63.8 %collective-permute-start.1 = (bf16[256,384]{1,0:T(8,128)(2,1)}, bf16[256,384]{1,0:T(8,128)(2,1)S(1)}, u32[]{:S(2)}, u32[]{:S(2)}) collective-permute-start(bf16[256,384]{1,0:T(8,128)(2,1)} %get-tuple-element.1643), channel_id=1, source_target_pairs={{1,0},{2,1},{3,2},{5,4},{6,5},{7,6},{9,8},{10,9},{11,10},{13,12},{... | collective-permute-start | bytes 589832 | tf_op jit(solution)/shard_map/while/body/eval_jaxpr/ppermute | solution.py:28
  911.5 72.9 %collective-permute-start.1 = (bf16[256,384]{1,0:T(8,128)(2,1)}, bf16[256,384]{1,0:T(8,128)(2,1)S(1)}, u32[]{:S(2)}, u32[]{:S(2)}) collective-permute-start(bf16[256,384]{1,0:T(8,128)(2,1)} %get-tuple-element.1643), channel_id=1, source_target_pairs={{1,0},{2,1},{3,2},{5,4},{6,5},{7,6},{9,8},{10,9},{11,10},{13,12},{... | collective-permute-start | bytes 589832 | tf_op jit(solution)/shard_map/while/body/eval_jaxpr/ppermute | solution.py:28
  1087.9 93.4 %collective-permute-start.1 = (bf16[256,384]{1,0:T(8,128)(2,1)}, bf16[256,384]{1,0:T(8,128)(2,1)S(1)}, u32[]{:S(2)}, u32[]{:S(2)}) collective-permute-start(bf16[256,384]{1,0:T(8,128)(2,1)} %get-tuple-element.1643), channel_id=1, source_target_pairs={{1,0},{2,1},{3,2},{5,4},{6,5},{7,6},{9,8},{10,9},{11,10},{13,12},{... | collective-permute-start | bytes 589832 | tf_op jit(solution)/shard_map/while/body/eval_jaxpr/ppermute | solution.py:28
  1110.9 70.4 %copy-start.60 = (f32[45,384]{1,0:T(8,128)S(1)}, f32[45,384]{1,0:T(8,128)}, u32[]{:S(2)}) copy-start(f32[45,384]{1,0:T(8,128)} %copy-done.59) | copy-start | bytes 207364 | tf_op jit(solution)/shard_map/while
  1111.0 70.4 %copy-start.147 = (s32[3]{0:T(128)S(1)}, s32[3]{0:T(128)}, u32[]{:S(2)}) copy-start(s32[3]{0:T(128)} %copy-done.146) | copy-start | bytes 40 | tf_op jit(solution)/shard_map/while
  1284.8 93.4 %collective-permute-start.1 = (bf16[256,384]{1,0:T(8,128)(2,1)}, bf16[256,384]{1,0:T(8,128)(2,1)S(1)}, u32[]{:S(2)}, u32[]{:S(2)}) collective-permute-start(bf16[256,384]{1,0:T(8,128)(2,1)} %get-tuple-element.1643), channel_id=1, source_target_pairs={{1,0},{2,1},{3,2},{5,4},{6,5},{7,6},{9,8},{10,9},{11,10},{13,12},{... | collective-permute-start | bytes 589832 | tf_op jit(solution)/shard_map/while/body/eval_jaxpr/ppermute | solution.py:28
  1307.9 70.4 %copy-start.60 = (f32[45,384]{1,0:T(8,128)S(1)}, f32[45,384]{1,0:T(8,128)}, u32[]{:S(2)}) copy-start(f32[45,384]{1,0:T(8,128)} %copy-done.59) | copy-start | bytes 207364 | tf_op jit(solution)/shard_map/while
  1307.9 70.4 %copy-start.147 = (s32[3]{0:T(128)S(1)}, s32[3]{0:T(128)}, u32[]{:S(2)}) copy-start(s32[3]{0:T(128)} %copy-done.146) | copy-start | bytes 40 | tf_op jit(solution)/shard_map/while
  1481.8 93.4 %collective-permute-start.1 = (bf16[256,384]{1,0:T(8,128)(2,1)}, bf16[256,384]{1,0:T(8,128)(2,1)S(1)}, u32[]{:S(2)}, u32[]{:S(2)}) collective-permute-start(bf16[256,384]{1,0:T(8,128)(2,1)} %get-tuple-element.1643), channel_id=1, source_target_pairs={{1,0},{2,1},{3,2},{5,4},{6,5},{7,6},{9,8},{10,9},{11,10},{13,12},{... | collective-permute-start | bytes 589832 | tf_op jit(solution)/shard_map/while/body/eval_jaxpr/ppermute | solution.py:28
  1504.9 70.4 %copy-start.147 = (s32[3]{0:T(128)S(1)}, s32[3]{0:T(128)}, u32[]{:S(2)}) copy-start(s32[3]{0:T(128)} %copy-done.146) | copy-start | bytes 40 | tf_op jit(solution)/shard_map/while
  1678.7 84.6 %collective-permute-start.1 = (bf16[256,384]{1,0:T(8,128)(2,1)}, bf16[256,384]{1,0:T(8,128)(2,1)S(1)}, u32[]{:S(2)}, u32[]{:S(2)}) collective-permute-start(bf16[256,384]{1,0:T(8,128)(2,1)} %get-tuple-element.1643), channel_id=1, source_target_pairs={{1,0},{2,1},{3,2},{5,4},{6,5},{7,6},{9,8},{10,9},{11,10},{13,12},{... | collective-permute-start | bytes 589832 | tf_op jit(solution)/shard_map/while/body/eval_jaxpr/ppermute | solution.py:28
  1775.9 316.5 %reduce-scatter.9.cloned.1.call-start = ((), (), s32[]{:S(2)}) async-start(), calls=%async_computation.8 | async-start | bytes 10616832 | tf_op jit(solution)/shard_map/reduce_scatter | solution.py:360
  1785.5 504.0 %reduce-scatter.11.cloned.1.call-start = ((), (), s32[]{:S(2)}) async-start(), calls=%async_computation.9 | async-start | bytes 13049856 | tf_op jit(solution)/shard_map/reduce_scatter | solution.py:361
  1798.0 553.7 %reduce-scatter.13.cloned.1.call-start = ((), (), s32[]{:S(2)}) async-start(), calls=%async_computation.11 | async-start | bytes 221184
  1799.7 632.3 %all-reduce.101.cloned.1.call-start = ((), (), s32[]{:S(2)}) async-start(), calls=%async_computation.17 | async-start | bytes 7028736 | tf_op jit(solution)/shard_map/psum | solution.py:364
  2289.5 284.4 %all-reduce.99.cloned.1.call-start = ((), (), s32[]{:S(2)}) async-start(), calls=%async_computation.16 | async-start | bytes 4718592 | tf_op jit(solution)/shard_map/psum | solution.py:380
  2462.2 236.4 %all-reduce.97.cloned.1.call-start = ((), (), s32[]{:S(2)}) async-start(), calls=%async_computation.15 | async-start | bytes 4718592 | tf_op jit(solution)/shard_map/psum | solution.py:390
  2590.3 231.1 %all-reduce.95.cloned.1.call-start = ((), (), s32[]{:S(2)}) async-start(), calls=%async_computation.14 | async-start | bytes 4718592 | tf_op jit(solution)/shard_map/psum | solution.py:390
  2713.1 231.1 %all-reduce.93.cloned.1.call-start = ((), (), s32[]{:S(2)}) async-start(), calls=%async_computation.13 | async-start | bytes 4718592 | tf_op jit(solution)/shard_map/psum | solution.py:390
  2835.9 232.2 %all-reduce.91.cloned.1.call-start = ((), (), s32[]{:S(2)}) async-start(), calls=%async_computation.12 | async-start | bytes 4718592 | tf_op jit(solution)/shard_map/psum | solution.py:390
  2958.7 113.8 %copy-start.85 = (f32[7456,48]{0,1:T(8,128)S(1)}, f32[7456,48]{0,1:T(8,128)}, u32[]{:S(2)}) copy-start(f32[7456,48]{0,1:T(8,128)} %param.35) | copy-start | bytes 4294660
  2958.7 138.1 %all-gather.11.cloned.1.call-start = ((), (), s32[]{:S(2)}) async-start(), calls=%async_computation.10 | async-start | bytes 1474560 | tf_op jit(solution)/shard_map/all_gather | solution.py:395
  (327 other events, 2165.7 us)
Sparse Core Ops, SparseCore 0:
  10.8 65.1 all-gather.6
  78.8 78.2 all-gather.8
  159.8 91.2 all-gather.4
  1776.0 150.1 reduce-scatter.6
  1930.0 162.3 reduce-scatter.8
  2096.3 193.2 reduce-scatter.10
  2293.3 58.2 reduce-scatter.12
  2354.2 77.7 all-reduce.100
  2462.3 111.6 all-reduce.98
  2590.4 108.0 all-reduce.96
  2713.2 108.1 all-reduce.94
  2836.0 108.1 all-reduce.92
  2958.8 109.2 all-reduce.90
  3072.6 20.5 all-gather.10
where the time goes:
time: 3130 us; the launch traced here: 3110 us
  waiting for transfers between devices  1620 us (52%)
  matrix products  505 us (16%)
  other arithmetic  322 us (10%)
  local copies, waits for them, and re-layouts  199 us (6%)
  starting transfers between devices  188 us (6%)
  loops' own time  132 us (4%)
  blocking collectives  119 us (4%)
    dot_general x192, matrix products, matmul(): jnp.dot(left, right, precision=highest, preferred_element_type=jnp.float32)  396 us
    psum x4, waiting for transfers between devices, body(): gram_pair = lax.psum((gram_of(own_attention), gram_of(own_feed)), 'dp')  390 us
    ppermute x12, waiting for transfers between devices, from_behind(): return lax.ppermute(shard, axis, pairs)  323 us
    reduce_scatter x1, waiting for transfers between devices, body(): lax.psum_scatter(grads[2], 'dp', scatter_dimension=1, tiled=True)  197 us
    ppermute x12, starting transfers between devices, from_behind(): return lax.ppermute(shard, axis, pairs)  186 us
    add x24, other arithmetic, backward_step(): total + jnp.where(valid, term, 0.0)  173 us
    reduce_scatter x1, waiting for transfers between devices, body(): lax.psum_scatter(grads[1], 'dp', scatter_dimension=2, tiled=True)  166 us
    reduce_scatter x1, waiting for transfers between devices, body(): lax.psum_scatter(grads[0], 'dp', scatter_dimension=2, tiled=True)  126 us
  transfers between devices with their start and end apart: 26, of which 25 were waited for; matrix products, arithmetic and copies ran while one was open for 8% of the time, Pallas kernels for 0%

commit v1 on v0

v1 whole, which is shorter than its diff:
```python
import functools
import math

import jax
import jax.numpy as jnp
import numpy as np
from jax import lax
from jax.experimental import pallas as pl
from jax.experimental.pallas import tpu as pltpu
from jax.sharding import PartitionSpec as P

HEADS = 6
HEAD = 64
LP = 304
KP = 384

highest = lax.Precision.HIGHEST
snr_gamma = 5.0
max_norm = 0.005
momentum_decay = 0.95
muon_rate = 0.05
adam_rate = 0.02
beta_one = 0.9
beta_two = 0.999
weight_decay = 0.01
coef_a = 3.4445
coef_b = -4.775
coef_c = 2.0315

f32, bf16 = jnp.float32, jnp.bfloat16
MESH = pl.DeviceIdType.MESH
ANY = pl.BlockSpec(memory_space=pl.ANY)
VM = pl.BlockSpec(memory_space=pltpu.VMEM)
SM = pl.BlockSpec(memory_space=pltpu.SMEM)
VMEM_LIMIT = 60000 * 1024


def low(value):
    return value.astype(bf16)


def nt(left, right):
    return lax.dot_general(left, right, (((1,), (1,)), ((), ())), preferred_element_type=f32)


def nn(left, right):
    return lax.dot_general(left, right, (((1,), (0,)), ((), ())), preferred_element_type=f32)


def tn(left, right):
    return lax.dot_general(left, right, (((0,), (0,)), ((), ())), preferred_element_type=f32)


def snr_weight(steps_t):
    level = jnp.cos((steps_t / 1000.0 + 0.008) / 1.008 * (math.pi / 2)) ** 2
    ratio = level / (1.0 - level)
    return level, jnp.minimum(ratio, snr_gamma) / ratio


def patchify(frames):
    clips, count, channels, height, breadth = frames.shape
    grid = frames.reshape(clips, count, channels, height // 2, 2, breadth // 2, 2)
    grid = grid.transpose(0, 1, 3, 5, 4, 6, 2)
    return grid.reshape(clips, count, (height // 2) * (breadth // 2), 4 * channels)


def sincos(places, model_width):
    half_width = model_width // 2
    freqs = np.exp(-math.log(10000.0) * np.arange(half_width) / half_width)
    angles = places[:, None] * freqs[None, :]
    return np.concatenate([np.sin(angles), np.cos(angles)], axis=1).astype(np.float32)


def col_sum(value):
    return jnp.sum(value.astype(f32), axis=0, keepdims=True)


def norm(value):
    centred = value - jnp.mean(value, axis=-1, keepdims=True)
    inv = lax.rsqrt(jnp.mean(centred * centred, axis=-1, keepdims=True) + 1e-06)
    return centred * inv, inv


def norm_back(grad, normed, inv):
    return inv * (
        grad
        - jnp.mean(grad, axis=-1, keepdims=True)
        - normed * jnp.mean(grad * normed, axis=-1, keepdims=True)
    )


GELU_C = math.sqrt(2.0 / math.pi)


def gelu(value):
    inner = GELU_C * (value + 0.044715 * (value * value * value))
    return value * (0.5 * (1.0 + jnp.tanh(inner)))


def gelu_both(value):
    square = value * value
    tanh = jnp.tanh(GELU_C * (value + 0.044715 * (square * value)))
    cdf = 0.5 * (1.0 + tanh)
    slope = 0.5 * (1.0 - tanh * tanh) * (GELU_C * (1.0 + 3 * 0.044715 * square))
    return value * cdf, cdf + value * slope


def lanes_low():
    lane = lax.broadcasted_iota(jnp.int32, (1, 128), 1)
    first = jnp.where(lane < HEAD, 1.0, 0.0)
    return low(first), low(1.0 - first), lane < HEAD


def stack_heads(pair, first, second):
    return jnp.concatenate([pair * first, pair * second], axis=0)


def attend(queries, keys, values, allowed):
    first, second, lower = lanes_low()
    rows = queries.shape[0]
    mixed, probs = [], []
    for pair in range(HEADS // 2):
        cut = slice(pair * 128, pair * 128 + 128)
        scores = nt(stack_heads(queries[:, cut], first, second), keys[:, cut]) * 0.125
        scores = jnp.where(allowed, scores, -1e30)
        weight = jnp.exp(scores - jnp.max(scores, axis=-1, keepdims=True))
        prob = weight / jnp.sum(weight, axis=-1, keepdims=True)
        probs.append(prob)
        out = nn(low(prob), values[:, cut])
        mixed.append(jnp.where(lower, out[:rows], out[rows:]))
    return low(jnp.concatenate(mixed, axis=1)), probs


def attend_back(grad, queries, keys, values, probs):
    first, second, lower = lanes_low()
    rows = queries.shape[0]
    dq, dk, dv = [], [], []
    for pair in range(HEADS // 2):
        cut = slice(pair * 128, pair * 128 + 128)
        stacked = stack_heads(grad[:, cut], first, second)
        prob = probs[pair]
        dv.append(tn(low(prob), stacked))
        dprob = nt(stacked, values[:, cut])
        dscore = low(prob * (dprob - jnp.sum(prob * dprob, axis=-1, keepdims=True)))
        part = nn(dscore, keys[:, cut])
        dq.append(jnp.where(lower, part[:rows], part[rows:]) * 0.125)
        dk.append(tn(dscore, stack_heads(queries[:, cut], first, second)) * 0.125)
    return tuple(jnp.concatenate(piece, axis=1) for piece in (dq, dk, dv))


def self_forward(x, mods, weights, bias, allowed):
    normed, inv = norm(x)
    a = low(normed * (1.0 + mods[1]) + mods[0])
    q = low(nt(a, weights[0]) + bias[0])
    k = low(nt(a, weights[1]))
    v = low(nt(a, weights[2]) + bias[1])
    o, probs = attend(q, k, v, allowed)
    branch = nt(o, weights[3]) + bias[2]
    return x + mods[2] * branch, (normed, inv, a, q, k, v, o, probs, branch)


def self_backward(dx, kept, mods, weights):
    normed, inv, a, q, k, v, o, probs, branch = kept
    dm2 = col_sum(dx * branch)
    dbr = low(dx * mods[2])
    do = low(nn(dbr, weights[3]))
    dq, dk, dv = (low(piece) for piece in attend_back(do, q, k, v, probs))
    da = nn(dq, weights[0]) + nn(dk, weights[1]) + nn(dv, weights[2])
    dm1, dm0 = col_sum(da * normed), col_sum(da)
    dx = dx + norm_back(da * (1.0 + mods[1]), normed, inv)
    return dx, (dm0, dm1, dm2), (col_sum(dq), col_sum(dv), col_sum(dbr)), (a, dq, dk, dv, o, dbr)


def feed_forward(x, mods, feed, bias_up, bias_down):
    normed, inv = norm(x)
    c = low(normed * (1.0 + mods[4]) + mods[3])
    u = nt(c, feed[0]) + bias_up
    g = low(gelu(u))
    branch = nn(g, feed[1]) + bias_down
    return x + mods[5] * branch, (normed, inv, c, u, g, branch)


def feed_backward(dx, kept, mods, feed):
    normed, inv, c, u, g, branch = kept
    dm5 = col_sum(dx * branch)
    dbr = low(dx * mods[5])
    du = low(nt(dbr, feed[1]) * gelu_both(u)[1])
    dc = nn(du, feed[0])
    dm4, dm3 = col_sum(dc * normed), col_sum(dc)
    dx = dx + norm_back(dc * (1.0 + mods[4]), normed, inv)
    return dx, (dm3, dm4, dm5), (col_sum(du), col_sum(dbr)), (c, dbr, du, g)


def pair_mask(kind):
    row = lax.broadcasted_iota(jnp.int32, (256, 128), 0) % 128
    col = lax.broadcasted_iota(jnp.int32, (256, 128), 1)
    if kind == 0:
        return row // 64 == col // 64
    return row % 32 == col % 32


VEC0, EMB0, HEAD0 = 0, 45, 61


def mod_rows(mq, vec, table, clip):
    rows = []
    for r in range(6):
        at = (r % 2) * 384
        rows.append(
            mq[r // 2, pl.ds(clip, 1), at : at + 384]
            + vec[3 + r : 4 + r]
            + vec[table + r : table + r + 1]
        )
    return rows


def up_bias(vec, start):
    return jnp.concatenate([vec[start + i : start + i + 1] for i in range(4)], axis=1)


def condition_kernel(rank, wt, ww, wm, perm, vec, hid, temb, mq, y2p):
    turned = jnp.transpose(ww[:, 1024:1152].astype(f32))
    vec[...] = turned
    feature = low(wt[:, 0:256])
    first = nt(feature, ww[:, 0:256]) + turned[1:2]
    hid[...] = first
    second = nt(low(first * jax.nn.sigmoid(first)), ww[:, 256:640]) + turned[2:3]
    temb[...] = second
    own = temb[pl.ds(pl.multiple_of(rank[0] * 8, 8), 8), :]
    mq[...] = nn(low(own * jax.nn.sigmoid(own)), wm[...])
    for h in range(2):
        y2p[h] = low(nt(ww[:, 640:1024], perm[h]))


def embed_chunk(tok_ref, vec, pos_ref, chunk):
    tokens = tok_ref[pl.ds(pl.multiple_of(chunk * 128, 128), 128), :]
    return low(nn(tokens, low(vec[...])) + (pos_ref[...] + vec[0:1])), tokens


def spatial_bias(vec):
    return (vec[11:12], vec[12:13], vec[13:14])


def first_kernel(role, half, tok, pos, mq, vec, wa, wf, wy, perm, captions, h1, hq, gq, cap, sems):
    @pl.when(role[0] == 1)
    def _():
        clips = captions.shape[0]
        for c in range(clips):
            pltpu.make_async_copy(captions.at[c], cap.at[c], sems.at[c]).start()
        bias = nt(low(vec[9:10]), perm[half[0]])
        for c in range(clips):
            pltpu.make_async_copy(captions.at[c], cap.at[c], sems.at[c]).wait()
            value = nt(cap[c], wy[...]) + bias
            rows = value.shape[0]
            pad = jnp.zeros((LP - rows, value.shape[1]), f32)
            hq[c] = jnp.concatenate([value, pad], axis=0)
            gq[c] = low(jnp.concatenate([gelu(value), pad], axis=0))

    @pl.when(role[0] == 0)
    def _():
        allowed = pair_mask(0)
        count = h1.shape[0]
        bu = up_bias(vec, 14)

        def step(chunk, carry):
            m = mod_rows(mq, vec, 19, (half[0] * count + chunk) // 2)
            h0, _ = embed_chunk(tok, vec, pos, chunk)
            x, _ = self_forward(h0.astype(f32), m, wa, spatial_bias(vec), allowed)
            x, _ = feed_forward(x, m, wf, bu, vec[18:19])
            out = low(x)
            for frame in range(2):
                for part in range(2):
                    start = frame * 64 + part * 32
                    h1[chunk, part, frame * 32 : frame * 32 + 32, :] = out[start : start + 32]
            return carry

        lax.fori_loop(0, count, step, 0)


def last_kernel(
    role, half, tok, pos, mq, vec, wa, wb, wf, dh, dkv, extra, grads_t, dmod_t,
    acts, actf, actw, dkvb, dy, vect, dmod, grads,
):
    @pl.when(role[0] == 0)
    def _():
        grads[...] = jnp.zeros_like(grads)
        dmod[...] = jnp.zeros_like(dmod)
        allowed = pair_mask(0)
        count = dh.shape[0]
        bu = up_bias(vec, 14)

        def step(chunk, carry):
            m = mod_rows(mq, vec, 19, (half[0] * count + chunk) // 2)
            h0, tokens = embed_chunk(tok, vec, pos, chunk)
            x, kept = self_forward(h0.astype(f32), m, wa, spatial_bias(vec), allowed)
            _, kept_f = feed_forward(x, m, wf, bu, vec[18:19])
            parts = []
            for frame in range(2):
                for part in range(2):
                    parts.append(dh[chunk, part, frame * 32 : frame * 32 + 32, :])
            dx = jnp.concatenate(parts, axis=0).astype(f32)
            dx, dm_f, db_f, act_f = feed_backward(dx, kept_f, m, wf)
            dx, dm_a, db_a, act_a = self_backward(dx, kept, m, wa)
            dh0 = low(dx)
            where = pl.ds(pl.multiple_of(chunk * 128, 128), 128)
            for i, value in enumerate(act_a):
                acts[i, where, :] = value
            for i in range(2):
                actf[i, where, :] = act_f[i]
                actw[i, where, :] = act_f[2 + i]
            mods = dm_a + dm_f
            dmod[chunk, 0:6, :] = jnp.concatenate(mods, axis=0)
            grads[...] += tn(tokens, dh0)
            grads[0:1] += col_sum(dh0)
            for i in range(3):
                grads[11 + i : 12 + i] += db_a[i]
            for i in range(4):
                grads[14 + i : 15 + i] += db_f[0][:, i * 384 : i * 384 + 384]
            grads[18:19] += db_f[1]
            for i in range(6):
                grads[19 + i : 20 + i] += mods[i]
            return carry

        lax.fori_loop(0, count, step, 0)

    @pl.when(role[0] == 1)
    def _():
        grads[...] = grads_t[...]
        dmod[...] = dmod_t[...]
        dy[...] = jnp.zeros_like(dy)
        dkvb[...] = jnp.zeros_like(dkvb)
        ncl = dy.shape[0]
        for c in range(ncl):

            @pl.when(jnp.logical_or(half[0] == 0, c > 0))
            def _():
                pieces = []
                for i in range(2):
                    value = dkv[i, c]
                    if c == ncl - 1:
                        value = value + jnp.where(half[0] == 0, extra[i], 0.0)
                    pieces.append(low(value))
                dkvb[0, c], dkvb[1, c] = pieces
                back = low(nn(pieces[0], wb[1]) + nn(pieces[1], wb[2]))
                dy[c] = back
                grads[40:41] += col_sum(pieces[1])
                grads[10:11] += col_sum(back)

    vect[...] = jnp.transpose(grads[...])


def temporal_kernel(
    role, half, rank, lens, errw, h1, timing, mq, vec, temb, wa, wb, wf, gq, y2p, target,
    dh1, acts, actf, actw, ybuf, dkv, grads, dmod, loss, kx, vx,
):
    @pl.when(role[0] == 0)
    def _():
        loss[...] = jnp.zeros_like(loss)

    @pl.when(role[0] == 1)
    def _():
        allowed = pair_mask(1)
        count = h1.shape[0]
        ncl = ybuf.shape[0]
        for ref in (kx, vx, dkv, grads, loss):
            ref[...] = jnp.zeros_like(ref)
        first_clip = (half[0] * count) // 2
        for c in range(ncl):
            clip = jnp.minimum(first_clip + c, gq.shape[1] - 1)
            y = low(nt(gq[0, clip], y2p[0]) + nt(gq[1, clip], y2p[1]) + vec[10:11])
            ybuf[c] = y
            kx[c, 0:LP, :] = low(nt(y, wb[1]))
            vx[c, 0:LP, :] = low(nt(y, wb[2]) + vec[40:41])
        bu = up_bias(vec, 28)
        lane = lax.broadcasted_iota(jnp.int32, (1, 128), 1)
        real = jnp.logical_and(lane >= HEAD0, lane < HEAD0 + 16)
        bias_h = pltpu.roll(jnp.broadcast_to(vec[44:45, 0:128], (8, 128)), HEAD0, 1)[0:1]
        head = low(vec[...])

        def step(chunk, carry):
            clip = (half[0] * count + chunk) // 2
            here = clip - first_clip
            m = mod_rows(mq, vec, 33, clip)
            emb = temb[pl.ds(rank[0] * 8 + clip, 1), :]
            m6, m7 = vec[42:43] + emb, vec[43:44] + emb
            h = jnp.concatenate([h1[chunk, 0], h1[chunk, 1]], axis=0)
            x = h.astype(f32) + timing[...]
            x, kept = self_forward(x, m, wa, (vec[25:26], vec[26:27], vec[27:28]), allowed)
            xb = low(x)
            cq = low(nt(xb, wb[0]) + vec[39:40])
            keys, values = kx[here], vx[here]
            seen = lax.broadcasted_iota(jnp.int32, (1, KP), 1) < lens[clip]
            co, probs = attend(cq, keys, values, seen)
            x = x + (nt(co, wb[3]) + vec[41:42])
            x, kept_f = feed_forward(x, m, wf, bu, vec[32:33])
            h2 = low(x).astype(f32)
            normed, inv = norm(h2)
            cf = low(normed * (1.0 + m7) + m6)
            where = pl.ds(pl.multiple_of(chunk * 128, 128), 128)
            diff = jnp.where(real, nt(cf, head) + bias_h - target[where, :], 0.0)
            scale = errw[clip]
            loss[...] += col_sum(diff * diff) * scale
            dpred = low(diff * (2.0 * scale))
            dcf = nn(dpred, head)
            grads[...] += tn(dpred, cf)
            dbh = pltpu.roll(jnp.broadcast_to(col_sum(dpred), (8, 128)), 128 - HEAD0, 1)[0:1]
            grads[44:45, 0:128] += dbh
            dm7, dm6 = col_sum(dcf * normed), col_sum(dcf)
            dx = low(norm_back(dcf * (1.0 + m7), normed, inv)).astype(f32)
            dx, dm_f, db_f, act_f = feed_backward(dx, kept_f, m, wf)
            dcbr = low(dx)
            dco = low(nn(dcbr, wb[3]))
            dcq, dck, dcv = attend_back(dco, cq, keys, values, probs)
            dcq = low(dcq)
            dkv[0, here] += dck[0:LP]
            dkv[1, here] += dcv[0:LP]
            dx = dx + nn(dcq, wb[0])
            dx, dm_a, db_a, act_a = self_backward(dx, kept, m, wa)
            out = low(dx)
            dh1[chunk, 0] = out[0:64]
            dh1[chunk, 1] = out[64:128]
            for i, value in enumerate(act_a + (xb, dcq, co, dcbr)):
                acts[i, where, :] = value
            for i in range(2):
                actf[i, where, :] = act_f[i]
                actw[i, where, :] = act_f[2 + i]
            mods = dm_a + dm_f + (dm6, dm7)
            dmod[chunk] = jnp.concatenate(mods, axis=0)
            for i in range(3):
                grads[25 + i : 26 + i] += db_a[i]
            for i in range(4):
                grads[28 + i : 29 + i] += db_f[0][:, i * 384 : i * 384 + 384]
            grads[32:33] += db_f[1]
            for i in range(6):
                grads[33 + i : 34 + i] += mods[i]
            grads[39:40] += col_sum(dcq)
            grads[41:42] += col_sum(dcbr)
            grads[42:43] += dm6
            grads[43:44] += dm7
            return carry

        lax.fori_loop(0, count, step, 0)


def weight_grad_kernel(
    role, half, acts_s, acts_t, racts, actf_s, actf_t, ractf, actw_s, actw_t, ractw,
    ybuf, rybuf, dkvb, rdkvb, dy, rdy, gq, hq, y2p, perm, captions,
    ga, gf, gy2, gy1, la, ra, lf, rf, lw, rw, cap, sems,
):
    side = ga.shape[1]
    six = acts_s.shape[0]

    def copies(r, h):
        if h == 0:
            local = acts_s if r == 0 else acts_t
            size = local.shape[0]
            return [
                (local, la.at[pl.ds(0, size)], 0),
                (racts.at[pl.ds(0, size)], ra.at[pl.ds(0, size)], 1),
            ]
        pick = ((actf_s, actw_s), (actf_t, actw_t))[r]
        return [(pick[0], lf, 0), (ractf, rf, 1), (pick[1], lw, 2), (ractw, rw, 3)]

    def text():
        return [(captions.at[c], cap.at[c], 4 + c) for c in range(captions.shape[0])]

    def run(group, finish):
        for src, dst, i in group:
            copy = pltpu.make_async_copy(src, dst, sems.at[i])
            copy.wait() if finish else copy.start()

    for r in range(2):
        for h in range(2):

            @pl.when(jnp.logical_and(role[0] == r, half[0] == h))
            def _():
                run(copies(r, h), False)
                if r == 1:
                    run(text(), False)
                run(copies(r, h), True)

    def both(i, j):
        return tn(la[i], la[j]) + tn(ra[i], ra[j])

    @pl.when(half[0] == 0)
    def _():
        for i in range(3):
            ga[i] = low(both(1 + i, 0))
        ga[3] = low(both(5, 4))

        @pl.when(role[0] == 1)
        def _():
            ga[4] = low(both(7, 6))
            for i in range(2):
                total = jnp.zeros((side, side), f32)
                for c in range(ybuf.shape[0]):
                    total = total + tn(dkvb[i, c], ybuf[c]) + tn(rdkvb[i, c], rybuf[c])
                ga[5 + i] = low(total)
            ga[7] = low(both(9, 8))

    @pl.when(half[0] == 1)
    def _():
        for pair in range(2):
            for tile in range(4):
                cut = slice(tile * 384, tile * 384 + 384)
                gf[pair, cut, :] = low(
                    tn(lw[pair, :, cut], lf[pair]) + tn(rw[pair, :, cut], rf[pair])
                )

    @pl.when(role[0] == 1)
    def _():
        clips = captions.shape[0]
        rows = captions.shape[1]
        owners = [((2 * c) // clips, c - (((2 * c) // clips) * clips) // 2) for c in range(clips)]

        def dy_of(c):
            h, at = owners[c]
            return jnp.where(half[0] == h, dy[at].astype(f32), rdy[at].astype(f32)).astype(bf16)

        @pl.when(half[0] == 1)
        def _():
            total = jnp.zeros((side, side), f32)
            for c in range(clips):
                plain = nn(gq[0, c], perm[0]) + nn(gq[1, c], perm[1])
                total = total + tn(dy_of(c), low(plain))
            gy2[...] = total

        turned = []
        sums = jnp.zeros((gy1.shape[0], 128), f32)
        ones = jnp.ones((rows, 128), bf16)
        for c in range(clips):
            back = nn(dy_of(c), y2p[half[0]]) * gelu_both(hq[c])[1]
            turned.append(low(jnp.transpose(back))[:, 0:rows])
            sums = sums + nn(turned[c], ones)
        run(text(), True)
        for tile in range(captions.shape[2] // 512):
            cut = slice(tile * 512, tile * 512 + 512)
            total = nn(turned[0], cap[0, :, cut])
            for c in range(1, clips):
                total = total + nn(turned[c], cap[c, :, cut])
            gy1[:, cut] = low(total)
        gy1[:, captions.shape[2] :] = low(sums)


def exact(left, right, dims):
    lh, rh = low(left), low(right)
    ll, rl = low(left - lh.astype(f32)), low(right - rh.astype(f32))

    def dot(a, b):
        return lax.dot_general(a, b, dims, preferred_element_type=f32)

    return dot(lh, rh) + (dot(lh, rl) + dot(ll, rh))


D_NN, D_NT, D_TN = ((((1,), (0,)), ((), ())), (((1,), (1,)), ((), ())), (((0,), (0,)), ((), ())))


def muon_kernel(half, ua, uf, xa, xf):
    @pl.when(half[0] == 0)
    def _():
        u = ua[...]
        x = u / (jnp.sqrt(jnp.sum(u * u)) + 1e-07)
        for sweep in range(5):
            gram = exact(x, x, D_NT)
            poly = coef_b * gram + coef_c * exact(gram, gram, D_NN)
            x = coef_a * x + exact(poly, x, D_NN)
        xa[...] = low(x)

    @pl.when(half[0] == 1)
    def _():
        width = uf.shape[1]
        tiles = uf.shape[0] // width
        gram = jnp.zeros((width, width), f32)
        for t in range(tiles):
            piece = uf[t * width : t * width + width, :]
            gram = gram + exact(piece, piece, D_TN)
        row = lax.broadcasted_iota(jnp.int32, (width, width), 0)
        col = lax.broadcasted_iota(jnp.int32, (width, width), 1)
        eye = jnp.where(row == col, 1.0, 0.0)
        inv = 1.0 / (jnp.sqrt(jnp.sum(gram * eye)) + 1e-07)
        gram = gram * (inv * inv)
        whole = None
        for sweep in range(5):
            poly = coef_a * eye + coef_b * gram + coef_c * exact(gram, gram, D_NN)
            whole = poly if whole is None else exact(poly, whole, D_NN)
            if sweep < 4:
                gram = exact(exact(poly, gram, D_NN), poly, D_NN)
        whole = whole * inv
        for t in range(tiles):
            cut = slice(t * width, t * width + width)
            xf[cut, :] = low(exact(uf[cut, :], whole, D_NN))


def local_call(kernel, out_shape, in_specs, args, scratch=()):
    return pl.pallas_call(
        kernel,
        out_shape=out_shape,
        in_specs=in_specs,
        out_specs=jax.tree.map(lambda _: VM, out_shape),
        scratch_shapes=scratch,
        compiler_params=pltpu.CompilerParams(vmem_limit_bytes=VMEM_LIMIT),
    )(*args)


def here():
    return lax.axis_index("dp"), lax.axis_index("segment")


def dev(d, s):
    return {"dp": d, "segment": s}


def remote(src, dst, send, recv, target):
    return pltpu.make_async_remote_copy(
        src_ref=src, dst_ref=dst, send_sem=send, recv_sem=recv, device_id=target,
        device_id_type=MESH,
    )


def greet(targets):
    barrier = pltpu.get_barrier_semaphore()
    for target in targets:
        pl.semaphore_signal(barrier, inc=1, device_id=target, device_id_type=MESH)
    pl.semaphore_wait(barrier, len(targets))


def greet_dp(n, extra=()):
    d, s = here()
    barrier = pltpu.get_barrier_semaphore()

    def step(k, carry):
        pl.semaphore_signal(
            barrier, inc=1, device_id=dev(lax.rem(d + k, n), s), device_id_type=MESH
        )
        return carry

    lax.fori_loop(1, n, step, 0)
    for target in extra:
        pl.semaphore_signal(barrier, inc=1, device_id=target, device_id_type=MESH)
    pl.semaphore_wait(barrier, n - 1 + len(extra))


def comm_call(kernel, cid, args, out_shape, sems):
    return pl.pallas_call(
        kernel,
        out_shape=out_shape,
        in_specs=[ANY] * len(args),
        out_specs=jax.tree.map(lambda _: ANY, out_shape),
        scratch_shapes=[pltpu.SemaphoreType.DMA(shape) for shape in sems],
        compiler_params=pltpu.CompilerParams(collective_id=cid, has_side_effects=True),
    )(*args)


def gather_kernel(n, pa, pb, pf, pw, py, pm, pt, wa, wb, wf, ww, wy, wm, wt,
                  send, recv, crecv, own):
    pair = 2 if n % 2 == 0 else 1
    line = n // pair
    d, s = here()
    role, half = s // 2, lax.rem(s, 2)
    a, x = d // pair, lax.rem(d, pair)
    mate = dev(d, role * 2 + 1 - half)
    above, below = dev(d + pair, s), dev(d - pair, s)
    across = dev(a * pair + (pair - 1 - x), s)
    barrier = pltpu.get_barrier_semaphore()

    def signal(target):
        pl.semaphore_signal(barrier, inc=1, device_id=target, device_id_type=MESH)

    signal(mate)
    if pair == 2:
        signal(across)

    @pl.when(a < line - 1)
    def _():
        signal(above)

    @pl.when(a > 0)
    def _():
        signal(below)

    pl.semaphore_wait(barrier, pair + jnp.minimum(a, 1) + jnp.minimum(line - 1 - a, 1))

    first = {
        0: {0: [(0, pa, wa, 4), (2, pw, ww, 0)], 1: [(0, pf, wf, 2)]},
        1: {0: [(0, pa, wa, 4), (1, pb, wb, 4), (2, pw, ww, 0)], 1: [(0, pf, wf, 2)]},
    }

    def slot(ref, lead, o):
        return ref.at[:, o] if lead else ref.at[o]

    for r in range(2):
        for h in range(2):

            @pl.when(jnp.logical_and(role == r, half == h))
            def _():
                parts = [(i, src, dst, lead, True) for i, src, dst, lead in first[r][h]]
                parts.append((3, pt, wt, 0, False))
                if (r, h) != (1, 1):
                    parts.append((4, pm, wm, 0, False))
                if r == 1:
                    parts.append((5, py, wy, 0, False))

                def move(part, way, o, target, is_own=False):
                    i, src, dst, lead, common = part
                    there = slot(dst, lead, o)
                    sem = crecv if way == 3 else recv
                    return remote(
                        src if is_own else there, there, send.at[way, i, o], sem.at[i, o], target
                    )

                def forward(o, up, down, side, is_own, finish):
                    def go(way, target):
                        for part in parts:
                            if way == 3 and not part[4]:
                                continue
                            copy = move(part, way, o, target, is_own)
                            copy.wait_send() if finish else copy.start()

                    if up is not None:
                        pl.when(up)(lambda: go(0, above))
                    if down is not None:
                        pl.when(down)(lambda: go(1, below))
                    if side and pair == 2:
                        go(2, across)
                    go(3, mate)

                def arrive(o):
                    for part in parts:
                        move(part, 0, o, across).wait_recv()

                for part in parts:
                    i, src, dst, lead, common = part
                    pltpu.make_async_copy(src, slot(dst, lead, d), own.at[i]).start()
                forward(d, a < line - 1, a > 0, True, True, False)
                other = pair - 1 - x

                def sweep(finish):
                    def step(k, carry):
                        @pl.when(a - k >= 0)
                        def _():
                            o = (a - k) * pair + x
                            if not finish:
                                arrive(o)
                            forward(o, a < line - 1, None, True, False, finish)

                        @pl.when(a + k < line)
                        def _():
                            o = (a + k) * pair + x
                            if not finish:
                                arrive(o)
                            forward(o, None, a > 0, True, False, finish)

                        if pair == 2:

                            @pl.when(a - (k - 1) >= 0)
                            def _():
                                o = (a - (k - 1)) * pair + other
                                if not finish:
                                    arrive(o)
                                forward(o, None, None, False, False, finish)

                            @pl.when(jnp.logical_and(k > 1, a + (k - 1) < line))
                            def _():
                                o = (a + (k - 1)) * pair + other
                                if not finish:
                                    arrive(o)
                                forward(o, None, None, False, False, finish)

                        return carry

                    lax.fori_loop(1, line + 1, step, 0)

                sweep(False)
                forward(d, a < line - 1, a > 0, True, True, True)
                sweep(True)
                for part in parts:
                    i, src, dst, lead, common = part
                    pltpu.make_async_copy(src, slot(dst, lead, d), own.at[i]).wait()

                def collect(o, carry):
                    for i, src, dst, lead in first[r][1 - h]:
                        there = slot(dst, lead, o)
                        remote(there, there, send.at[3, i, o], crecv.at[i, o], mate).wait_recv()
                    return carry

                lax.fori_loop(0, n, collect, 0)


def segment_kernel(count, *refs):
    ins, outs = refs[:count], refs[count : 2 * count]
    send, recv, own = refs[2 * count :]
    d, s = here()
    peers = [dev(d, lax.rem(s + k, 4)) for k in range(1, 4)]
    greet(peers)
    for i in range(count):
        pltpu.make_async_copy(ins[i], outs[i].at[s], own.at[i]).start()
        for k in range(1, 4):
            remote(ins[i], outs[i].at[s], send.at[i, k], recv.at[i, k], peers[k - 1]).start()
    for i in range(count):
        pltpu.make_async_copy(ins[i], outs[i].at[s], own.at[i]).wait()
        for k in range(1, 4):
            o = lax.rem(s + 4 - k, 4)
            remote(ins[i], outs[i].at[o], send.at[i, k], recv.at[i, k], dev(d, o)).wait()


def segment_exchange(cid, arrays):
    shapes = [jax.ShapeDtypeStruct((4,) + a.shape, a.dtype) for a in arrays]
    k = len(arrays)
    return comm_call(
        functools.partial(segment_kernel, k), cid, arrays, shapes, [(k, 4), (k, 4), (k,)]
    )


def dp_gather_kernel(n, src, dst, send, recv, own):
    d, s = here()
    greet_dp(n)
    pltpu.make_async_copy(src, dst.at[d], own.at[0]).start()

    def start(k, carry):
        remote(src, dst.at[d], send.at[k], recv.at[k], dev(lax.rem(d + k, n), s)).start()
        return carry

    def finish(k, carry):
        o = lax.rem(d + n - k, n)
        remote(src, dst.at[o], send.at[k], recv.at[k], dev(o, s)).wait()
        return carry

    lax.fori_loop(1, n, start, 0)
    lax.fori_loop(1, n, finish, 0)
    pltpu.make_async_copy(src, dst.at[d], own.at[0]).wait()


def forward_kernel(count, h1s, gq, h1t, gqs, send, recv, msend, mrecv):
    relay_half_clips(count, 0, h1s, h1t, send, recv, None, (gq, gqs, msend, mrecv))


def relay_half_clips(count, from_role, src, dst, send, recv, extra, swap=None):
    d, s = here()
    role, half = s // 2, lax.rem(s, 2)
    peers = [dev(d, (1 - role) * 2), dev(d, (1 - role) * 2 + 1)]
    mate = dev(d, role * 2 + 1 - half)
    peers.append(mate)
    greet(peers)

    def unit(i, part):
        there = half * count + i
        clip, own = there // 2, lax.rem(there, 2)
        other = 2 * clip + part
        return own, other // count, lax.rem(other, count)

    def copy(i, part):
        own, to, slot = unit(i, part)
        return remote(
            src.at[i, part], dst.at[slot, own], send.at[i, part], recv.at[slot, own],
            dev(d, (1 - from_role) * 2 + to),
        )

    if swap is not None:
        mine, both, msend, mrecv = swap

        @pl.when(role == 1)
        def _():
            pltpu.make_async_copy(mine, both.at[half], msend.at[1]).start()
            remote(mine, both.at[half], msend.at[0], mrecv.at[0], mate).start()

    if extra is not None:
        own_src, own_dst, esend, erecv = extra

        @pl.when(jnp.logical_and(role == 1, half == 1))
        def _():
            remote(own_src, own_dst, esend.at[0], erecv.at[0], dev(d, 2)).start()

    @pl.when(role == from_role)
    def _():
        for i in range(count):
            for part in range(2):
                copy(i, part).start()
        for i in range(count):
            for part in range(2):
                copy(i, part).wait_send()

    @pl.when(role == 1 - from_role)
    def _():
        for i in range(count):
            for part in range(2):
                remote(
                    src.at[i, part], dst.at[i, part], send.at[i, part], recv.at[i, part],
                    dev(d, from_role * 2),
                ).wait_recv()

    if swap is not None:

        @pl.when(role == 1)
        def _():
            pltpu.make_async_copy(mine, both.at[half], msend.at[1]).wait()
            remote(mine, both.at[1 - half], msend.at[0], mrecv.at[0], mate).wait()

    if extra is not None:

        @pl.when(jnp.logical_and(role == 1, half == 1))
        def _():
            remote(own_src, own_dst, esend.at[0], erecv.at[0], dev(d, 2)).wait_send()

        @pl.when(jnp.logical_and(role == 1, half == 0))
        def _():
            remote(own_src, own_dst, esend.at[0], erecv.at[0], dev(d, 2)).wait_recv()


def backward_kernel(count, dh1, dkv, dhs, extra, send, recv, esend, erecv):
    relay_half_clips(
        count, 1, dh1, dhs, send, recv, (dkv.at[:, 0], extra, esend, erecv)
    )


def swap_kernel(acts_s, acts_t, actf_s, actf_t, actw_s, actw_t, ybuf, dkvb, dy, dmod,
                racts, ractf, ractw, rybuf, rdkvb, rdy, dmods,
                send, recv, send_all, recv_all, own):
    d, s = here()
    role, half = s // 2, lax.rem(s, 2)
    peers = [dev(d, lax.rem(s + k, 4)) for k in range(1, 4)]
    greet(peers)
    mate = dev(d, role * 2 + 1 - half)
    six = acts_s.shape[0]
    pltpu.make_async_copy(dmod, dmods.at[s], own.at[0]).start()
    for k in range(1, 4):
        remote(dmod, dmods.at[s], send_all.at[k], recv_all.at[k], peers[k - 1]).start()
    gives = {
        (0, 0): [(0, actf_s, ractf), (1, actw_s, ractw)],
        (0, 1): [(0, acts_s, racts.at[pl.ds(0, six)])],
        (1, 0): [(0, actf_t, ractf), (1, actw_t, ractw), (2, dy, rdy)],
        (1, 1): [(0, acts_t, racts), (1, ybuf, rybuf), (3, dkvb, rdkvb), (2, dy, rdy)],
    }
    for (r, h), mine in gives.items():

        @pl.when(jnp.logical_and(role == r, half == h))
        def _():
            for i, src, dst in mine:
                remote(src, dst, send.at[i], recv.at[i], mate).start()
            for i, src, dst in mine:
                remote(src, dst, send.at[i], recv.at[i], mate).wait_send()
            for i, src, dst in gives[(r, 1 - h)]:
                remote(src, dst, send.at[i], recv.at[i], mate).wait_recv()

    pltpu.make_async_copy(dmod, dmods.at[s], own.at[0]).wait()
    for k in range(1, 4):
        o = lax.rem(s + 4 - k, 4)
        remote(dmod, dmods.at[o], send_all.at[k], recv_all.at[k], dev(d, o)).wait()


def scatter_kernel(n, ga, gf, gy2, gy1, dm, vec, ra, rf, ry2, ry1, rm, rv, send, recv, own):
    d, s = here()
    role, half = s // 2, lax.rem(s, 2)
    greet_dp(n)

    def parts(r, h):
        if h == 0:
            if r == 0:
                first = [(0, lambda p: ga.at[pl.ds(0, 4), p], lambda o: ra.at[o, pl.ds(0, 4)])]
            else:
                first = [(0, lambda p: ga.at[:, p], lambda o: ra.at[o])]
        else:
            first = [(0, lambda p: gf.at[:, p], lambda o: rf.at[o])]
            if r == 1:
                first.append((1, lambda p: gy2.at[p], lambda o: ry2.at[o]))
        if r == 1:
            first.append((2, lambda p: gy1.at[p], lambda o: ry1.at[o]))
        return first + [
            (3, lambda p: dm, lambda o: rm.at[o]),
            (4, lambda p: vec.at[p], lambda o: rv.at[o]),
        ]

    for r in range(2):
        for h in range(2):

            @pl.when(jnp.logical_and(role == r, half == h))
            def _():
                group = parts(r, h)
                for i, src, dst in group:
                    pltpu.make_async_copy(src(d), dst(d), own.at[i]).start()

                def start(k, carry):
                    to = lax.rem(d + k, n)
                    for i, src, dst in group:
                        remote(src(to), dst(d), send.at[i, k], recv.at[i, k], dev(to, s)).start()
                    return carry

                def finish(k, carry):
                    o = lax.rem(d + n - k, n)
                    for i, src, dst in group:
                        remote(src(o), dst(o), send.at[i, k], recv.at[i, k], dev(o, s)).wait()
                    return carry

                lax.fori_loop(1, n, start, 0)
                lax.fori_loop(1, n, finish, 0)
                for i, src, dst in group:
                    pltpu.make_async_copy(src(d), dst(d), own.at[i]).wait()


def middle_kernel(n, dtemb, vec, tile, dtembs, vecs, tiles, send, recv, send_all, recv_all, own):
    d, s = here()
    peers = [dev(d, lax.rem(s + k, 4)) for k in range(1, 4)]
    greet_dp(n, peers)
    pltpu.make_async_copy(dtemb, dtembs.at[d], own.at[0]).start()

    def start(k, carry):
        remote(dtemb, dtembs.at[d], send.at[k], recv.at[k], dev(lax.rem(d + k, n), s)).start()
        return carry

    def finish(k, carry):
        o = lax.rem(d + n - k, n)
        remote(dtemb, dtembs.at[o], send.at[k], recv.at[k], dev(o, s)).wait()
        return carry

    lax.fori_loop(1, n, start, 0)
    pairs = [(0, vec, vecs), (1, tile, tiles)]
    for i, src, dst in pairs:
        pltpu.make_async_copy(src, dst.at[s], own.at[1 + i]).start()
        for k in range(1, 4):
            remote(src, dst.at[s], send_all.at[i, k], recv_all.at[i, k], peers[k - 1]).start()
    for i, src, dst in pairs:
        pltpu.make_async_copy(src, dst.at[s], own.at[1 + i]).wait()
        for k in range(1, 4):
            o = lax.rem(s + 4 - k, 4)
            remote(src, dst.at[o], send_all.at[i, k], recv_all.at[i, k], dev(d, o)).wait()
    lax.fori_loop(1, n, finish, 0)
    pltpu.make_async_copy(dtemb, dtembs.at[d], own.at[0]).wait()


class Relay:
    def __init__(self, send, recv):
        self.d, self.s = here()
        self.role, self.half = self.s // 2, lax.rem(self.s, 2)
        self.other = dev(self.d, (1 - self.role) * 2 + self.half)
        self.mate = dev(self.d, self.role * 2 + 1 - self.half)
        self.send, self.recv = send, recv

    def at(self, r, h):
        return jnp.logical_and(self.role == r, self.half == h)

    def copy(self, i, leg, src, dst):
        target = self.other if leg == 0 else self.mate
        return remote(src, dst, self.send.at[i, leg], self.recv.at[i, leg], target)

    def start(self, i, src, dst):
        self.copy(i, 0, src, dst).start()
        self.copy(i, 1, src, dst).start()

    def middle(self, i, dst):
        self.copy(i, 0, dst, dst).wait_recv()
        self.copy(i, 2, dst, dst).start()

    def finish(self, r, h, items):
        @pl.when(self.at(r, h))
        def _():
            for i, src, dst in items:
                self.copy(i, 0, src, dst).wait_send()
                self.copy(i, 1, src, dst).wait_send()

        @pl.when(self.at(1 - r, h))
        def _():
            for i, src, dst in items:
                self.copy(i, 2, dst, dst).wait_send()

        @pl.when(self.at(r, 1 - h))
        def _():
            for i, src, dst in items:
                self.copy(i, 1, dst, dst).wait_recv()

        @pl.when(self.at(1 - r, 1 - h))
        def _():
            for i, src, dst in items:
                self.copy(i, 2, dst, dst).wait_recv()


def owner_first(role, mat):
    return 2 * mat + mat % 2 if role == 0 else mat


def owner_second(mat):
    return 2 + 3 * mat


def collect_kernel(n, ua, uf, ga, gf, gy1, gy2, oa, of, xa, xf, xy1, xy2,
                   send, recv, own, gsend, grecv, gown):
    relay = Relay(gsend, grecv)
    d, s, role, half = relay.d, relay.s, relay.role, relay.half
    greet_dp(n, [relay.other, relay.mate])
    four = pl.ds(0, 4)
    shared = {
        (0, 0): [(0, ga.at[four], xa.at[0, four])],
        (0, 1): [(1, gf, xf.at[0])],
        (1, 0): [(2, ga, xa.at[1]), (3, gy1, xy1.at[0])],
        (1, 1): [(4, gf, xf.at[1]), (5, gy1, xy1.at[1]), (6, gy2, xy2)],
    }
    groups = []
    for r in range(2):
        mats = 4 if r == 0 else 8
        groups.append((r, 0, [(m, owner_first(r, m), ua.at[m], oa) for m in range(mats)]))
        groups.append((r, 1, [(m, owner_second(m), uf.at[m], of) for m in range(2)]))
    for r, h, mats in groups:

        @pl.when(relay.at(r, h))
        def _():
            for m, o, src, dst in mats:

                @pl.when(d == o)
                def _():
                    pltpu.make_async_copy(src, dst.at[d], own.at[0]).start()

                @pl.when(d != o)
                def _():
                    remote(src, dst.at[d], send.at[m], recv.at[d], dev(o, s)).start()

            for i, src, dst in shared[(r, h)]:
                pltpu.make_async_copy(src, dst, gown.at[i]).start()
                relay.start(i, src, dst)

    for (r, h), items in shared.items():

        @pl.when(relay.at(1 - r, h))
        def _():
            for i, src, dst in items:
                relay.middle(i, dst)

    for r, h, mats in groups:

        @pl.when(relay.at(r, h))
        def _():
            for i, src, dst in shared[(r, h)]:
                pltpu.make_async_copy(src, dst, gown.at[i]).wait()
            for m, o, src, dst in mats:

                @pl.when(d == o)
                def _():
                    pltpu.make_async_copy(src, dst.at[d], own.at[0]).wait()

                    def finish(k, carry):
                        p = lax.rem(d + n - k, n)
                        remote(src, dst.at[p], send.at[m], recv.at[p], dev(p, s)).wait_recv()
                        return carry

                    lax.fori_loop(1, n, finish, 0)

                @pl.when(d != o)
                def _():
                    remote(src, dst.at[d], send.at[m], recv.at[d], dev(o, s)).wait_send()

    for (r, h), items in shared.items():
        relay.finish(r, h, items)


def spread_kernel(n, xa, xf, oa, of, send, recv, rsend, rrecv, own):
    relay = Relay(rsend, rrecv)
    d, s, role, half = relay.d, relay.s, relay.role, relay.half
    greet_dp(n, [relay.other, relay.mate])
    groups = []
    for r in range(2):
        mats = 4 if r == 0 else 8
        groups.append((r, 0, mats, functools.partial(owner_first, r), xa, oa, 10 * r))
        groups.append((r, 1, 2, owner_second, xf, of, 10 * r + 8))
    for r, h, mats, owner, src, dst, base in groups:

        @pl.when(relay.at(r, h))
        def _():
            for m in range(mats):

                @pl.when(d == owner(m))
                def _():
                    pltpu.make_async_copy(src.at[d], dst.at[r, m], own.at[m]).start()

                    def start(k, carry):
                        to = lax.rem(d + k, n)
                        remote(
                            src.at[to], dst.at[r, m], send.at[k], recv.at[m], dev(to, s)
                        ).start()
                        return carry

                    lax.fori_loop(1, n, start, 0)

            for m in range(mats):

                @pl.when(d == owner(m))
                def _():
                    pltpu.make_async_copy(src.at[d], dst.at[r, m], own.at[m]).wait()

                @pl.when(d != owner(m))
                def _():
                    remote(
                        src.at[d], dst.at[r, m], send.at[1], recv.at[m], dev(owner(m), s)
                    ).wait_recv()

                relay.start(base + m, dst.at[r, m], dst.at[r, m])

    for r, h, mats, owner, src, dst, base in groups:

        @pl.when(relay.at(1 - r, h))
        def _():
            for m in range(mats):
                relay.middle(base + m, dst.at[r, m])

    for r, h, mats, owner, src, dst, base in groups:

        @pl.when(relay.at(r, h))
        def _():
            for m in range(mats):

                @pl.when(d == owner(m))
                def _():
                    def finish(k, carry):
                        to = lax.rem(d + k, n)
                        remote(
                            src.at[to], dst.at[r, m], send.at[k], recv.at[m], dev(to, s)
                        ).wait_send()
                        return carry

                    lax.fori_loop(1, n, finish, 0)

        relay.finish(r, h, [(base + m, dst.at[r, m], dst.at[r, m]) for m in range(mats)])


def adamw_update(weight, first, second, grad, count):
    first = beta_one * first + (1.0 - beta_one) * grad
    second = beta_two * second + (1.0 - beta_two) * grad * grad
    first_hat = first / (1.0 - jnp.power(beta_one, count))
    second_hat = second / (1.0 - jnp.power(beta_two, count))
    weight = weight - adam_rate * (
        first_hat / (jnp.sqrt(second_hat) + 1e-08) + weight_decay * weight
    )
    return (weight, first, second)


def silu_slope(value):
    gate = jax.nn.sigmoid(value)
    return gate * (1.0 + value * (1.0 - gate))


def dot32(left, right, dims):
    return lax.dot_general(left, right, (dims, ((), ())), precision=highest)


def body(
    latents,
    noise_draw,
    timesteps,
    captions,
    caption_len,
    attention_weights,
    feed_weights,
    side_weights,
    vector_weights,
    attention_momentum,
    feed_momentum,
    side_first,
    side_second,
    vector_first,
    vector_second,
    step_count,
):
    n = lax.axis_size("dp")
    d, s = here()
    role, half = s // 2, lax.rem(s, 2)
    count = latents.shape[0]
    frames = latents.shape[1]
    width = attention_weights.shape[1]
    cols, feed_cols = attention_weights.shape[2], feed_weights.shape[2]
    hidden = n * feed_cols
    text = captions.shape[2]
    sds = jax.ShapeDtypeStruct
    role_s, half_s = role.reshape(1).astype(jnp.int32), half.reshape(1).astype(jnp.int32)

    o_time = 16
    o_text = o_time + 256 + width
    o_text2 = o_text + text
    o_head = o_text2 + width
    o_mod = o_head + 16
    six = 6 * width
    own_rows = -(-cols // 2)
    lanes = n * own_rows

    perm_np = np.zeros((2, lanes, width), np.float32)
    for h in range(width):
        origin, col = divmod(h, cols)
        perm_np[col // own_rows, origin * own_rows + col % own_rows, h] = 1.0
    perm = jnp.asarray(perm_np, bf16)

    att_t = jnp.swapaxes(attention_weights, 1, 2)
    feed_t = jnp.swapaxes(feed_weights, 1, 2)
    side_t = side_weights.T
    side_b = low(side_t)
    pa = low(lax.dynamic_slice_in_dim(att_t, 4 * role, 4, 0))
    pb = low(att_t[8:12])
    pf = low(lax.dynamic_slice_in_dim(feed_t, 2 * role, 2, 0))
    pw = jnp.concatenate(
        [
            side_b[:, o_time:o_text],
            side_b[:, o_text2:o_head],
            low(vector_weights.T),
            side_b[:, 0:16],
            side_b[:, o_head:o_mod],
            jnp.zeros((cols, 128 - 77), bf16),
        ],
        axis=1,
    )
    text_rows = jnp.pad(side_b[:, o_text:o_text2], ((0, 2 * own_rows - cols), (0, 0)))
    py = lax.dynamic_slice_in_dim(text_rows, half * own_rows, own_rows, 0)
    pm = lax.dynamic_slice_in_dim(side_b[:, o_mod:], jnp.minimum(s, 2) * 2 * width, 2 * width, 1)
    freqs = jnp.exp(-math.log(10000.0) * jnp.arange(128, dtype=f32) / 128)
    angles = timesteps.astype(f32)[:, None] * freqs[None, :]
    level, snr = snr_weight(timesteps.astype(f32))
    pt = jnp.concatenate([jnp.cos(angles), jnp.sin(angles), snr[:, None]], axis=1)
    pt = jnp.pad(pt, ((0, 8 - count), (0, width - 257)))

    wa, wb, wf, ww, wy, wm, wt = comm_call(
        functools.partial(gather_kernel, n),
        1,
        (pa, pb, pf, pw, py, pm, pt),
        [
            sds((4, n, cols, width), bf16),
            sds((4, n, cols, width), bf16),
            sds((2, n, feed_cols, width), bf16),
            sds((n, cols, 1152), bf16),
            sds((n, own_rows, text), bf16),
            sds((n, cols, 2 * width), bf16),
            sds((n, 8, width), f32),
        ],
        [(4, 6, n), (6, n), (6, n), (6,)],
    )
    wa = wa.reshape(4, width, width)
    wb = wb.reshape(4, width, width)
    wf = wf.reshape(2, hidden, width)
    ww = ww.reshape(width, 1152)
    wy = wy.reshape(lanes, text)
    wm = wm.reshape(width, 2 * width)
    total_weight = jnp.sum(wt[:, :, 256])

    rank_s = d.reshape(1).astype(jnp.int32)
    vec, hid, temb, mq_own, y2p = local_call(
        condition_kernel,
        [
            sds((128, width), f32),
            sds((n * 8, width), f32),
            sds((n * 8, width), f32),
            sds((8, 2 * width), f32),
            sds((2, width, lanes), bf16),
        ],
        [SM] + [VM] * 4,
        (rank_s, wt.reshape(n * 8, width), ww, wm, perm),
    )
    (mq,) = segment_exchange(2, (mq_own,))

    level = level[:, None, None, None, None]
    noisy = low(jnp.sqrt(level) * latents + jnp.sqrt(1.0 - level) * noise_draw).astype(f32)
    patches = patchify(jnp.where(role == 0, noisy, noise_draw))
    per_clip = frames * patches.shape[2]
    half_tokens = count * per_clip // 2
    regrouped = patches.reshape(count, frames, 2, 32, 16).transpose(0, 2, 1, 3, 4)
    regrouped = regrouped.reshape(count * per_clip, 16)
    rows = jnp.where(role == 0, patches.reshape(count * per_clip, 16), regrouped)
    rows = lax.dynamic_slice_in_dim(rows, half * half_tokens, half_tokens, 0)
    tok = low(jnp.pad(rows, ((0, 0), (EMB0, 112 - EMB0))))
    target = jnp.pad(rows, ((0, 0), (HEAD0, 112 - HEAD0)))
    places = np.arange(patches.shape[2])
    edge = latents.shape[3] // 2
    pos = np.concatenate(
        [sincos(places // edge, width // 2), sincos(places % edge, width // 2)], axis=1
    )
    pos = jnp.asarray(np.tile(pos, (2, 1)))
    timing = jnp.asarray(np.repeat(sincos(np.arange(frames), width), 32, axis=0))

    clip_rows = captions.shape[1]
    h1s, hq, gq_own = local_call(
        first_kernel,
        [
            sds((count, 2, 64, width), bf16),
            sds((count, LP, lanes), f32),
            sds((count, LP, lanes), bf16),
        ],
        [SM] * 2 + [VM] * 8 + [ANY],
        (role_s, half_s, tok, pos, mq, vec, wa, wf, wy, perm, captions),
        [pltpu.VMEM((count, clip_rows, text), bf16), pltpu.SemaphoreType.DMA((count,))],
    )
    h1t, gq = comm_call(
        functools.partial(forward_kernel, count),
        3,
        (h1s, gq_own),
        [sds((count, 2, 64, width), bf16), sds((2, count, LP, lanes), bf16)],
        [(count, 2), (count, 2), (2,), (1,)],
    )

    ncl = (count + 1) // 2
    errw = snr / (total_weight * (per_clip * 16.0))
    wide = sds((2, half_tokens, hidden), bf16)
    thin = sds((2, half_tokens, width), bf16)
    cap_like = sds((ncl, LP, width), bf16)
    dh1, acts_t, actf_t, actw_t, ybuf, dkv, grads_t, dmod_t, loss_t = local_call(
        temporal_kernel,
        [
            sds((count, 2, 64, width), bf16),
            sds((10, half_tokens, width), bf16),
            thin,
            wide,
            cap_like,
            sds((2, ncl, LP, width), f32),
            sds((128, width), f32),
            sds((count, 8, width), f32),
            sds((1, 128), f32),
        ],
        [SM] * 5 + [VM] * 11,
        (
            role_s, half_s, rank_s, caption_len, errw, h1t, timing, mq, vec, temb, wa, wb, wf, gq,
            y2p, target,
        ),
        [pltpu.VMEM((ncl, KP, width), bf16), pltpu.VMEM((ncl, KP, width), bf16)],
    )
    dhs, extra = comm_call(
        functools.partial(backward_kernel, count),
        4,
        (dh1, dkv),
        [sds((count, 2, 64, width), bf16), sds((2, LP, width), f32)],
        [(count, 2), (count, 2), (1,), (1,)],
    )
    acts_s, actf_s, actw_s, dkvb, dy, vect, dmod = local_call(
        last_kernel,
        [
            sds((6, half_tokens, width), bf16),
            thin,
            wide,
            sds((2, ncl, LP, width), bf16),
            cap_like,
            sds((width, 128), f32),
            sds((count, 8, width), f32),
        ],
        [SM] * 2 + [VM] * 12,
        (role_s, half_s, tok, pos, mq, vec, wa, wb, wf, dhs, dkv, extra, grads_t, dmod_t),
        [pltpu.VMEM((128, width), f32)],
    )
    racts, ractf, ractw, rybuf, rdkvb, rdy, dmods = comm_call(
        swap_kernel,
        5,
        (acts_s, acts_t, actf_s, actf_t, actw_s, actw_t, ybuf, dkvb, dy, dmod),
        [
            sds((10, half_tokens, width), bf16),
            thin,
            wide,
            cap_like,
            sds((2, ncl, LP, width), bf16),
            cap_like,
            sds((4, count, 8, width), f32),
        ],
        [(4,), (4,), (4,), (4,), (1,)],
    )
    ga, gf, gy2, gy1 = local_call(
        weight_grad_kernel,
        [
            sds((8, width, width), bf16),
            sds((2, hidden, width), bf16),
            sds((width, width), f32),
            sds((lanes, text + 128), bf16),
        ],
        [SM] * 2 + [ANY] * 9 + [VM] * 10 + [ANY],
        (
            role_s, half_s, acts_s, acts_t, racts, actf_s, actf_t, ractf, actw_s, actw_t, ractw,
            ybuf, rybuf, dkvb, rdkvb, dy, rdy, gq, hq, y2p, perm, captions,
        ),
        [
            pltpu.VMEM((10, half_tokens, width), bf16),
            pltpu.VMEM((10, half_tokens, width), bf16),
            pltpu.VMEM(thin.shape, bf16),
            pltpu.VMEM(thin.shape, bf16),
            pltpu.VMEM(wide.shape, bf16),
            pltpu.VMEM(wide.shape, bf16),
            pltpu.VMEM((count, clip_rows, text), bf16),
            pltpu.SemaphoreType.DMA((4 + count,)),
        ],
    )

    dm_clip = []
    for clip in range(count):
        total = 0.0
        for seg in range(4):
            for i in range(count):
                if ((seg % 2) * count + i) // 2 == clip:
                    total = total + dmods[seg, i]
        dm_clip.append(total)
    dm = jnp.concatenate(dm_clip, axis=0)

    ra, rf, ry2, ry1, rm, rv = comm_call(
        functools.partial(scatter_kernel, n),
        6,
        (
            ga.reshape(8, n, cols, width),
            gf.reshape(2, n, feed_cols, width),
            gy2.reshape(n, cols, width),
            gy1.reshape(n, own_rows, text + 128),
            dm,
            vect.reshape(n, cols, 128),
        ),
        [
            sds((n, 8, cols, width), bf16),
            sds((n, 2, feed_cols, width), bf16),
            sds((n, cols, width), f32),
            sds((n, own_rows, text + 128), bf16),
            sds((n, 8 * count, width), f32),
            sds((n, cols, 128), f32),
        ],
        [(5, n), (5, n), (5,)],
    )
    mats = jnp.arange(8)[:, None, None]
    real = jnp.logical_and(half == 0, jnp.logical_or(role == 1, mats < 4))
    grad_a = jnp.where(real, jnp.sum(ra.astype(f32), axis=0), 0.0)
    grad_f = jnp.where(half == 1, jnp.sum(rf.astype(f32), axis=0), 0.0)
    grad_y2 = jnp.where(s == 3, jnp.sum(ry2, axis=0), 0.0)
    valid = half * own_rows + jnp.arange(own_rows)[:, None] < cols
    grad_y1 = jnp.where(jnp.logical_and(role == 1, valid), jnp.sum(ry1.astype(f32), axis=0), 0.0)
    grad_v = jnp.sum(rv, axis=0)

    per = rm.reshape(n * count, 8, width)
    dmod_all = per[:, :6].reshape(n * count, six)
    wm_own = side_b[:, o_mod:]

    def own_cols(value):
        return lax.dynamic_slice_in_dim(value, d * cols, cols, value.ndim - 1)

    def clips_of(value):
        return value.reshape(n, 8, -1)[:, :count].reshape(n * count, -1)

    hid_all, temb_all = clips_of(hid), clips_of(temb)
    feature = low(clips_of(wt.reshape(n * 8, width))[:, :256])
    sh_all = low(jax.nn.silu(hid_all))
    temb_own = own_cols(temb_all)
    dsil = dot32(dmod_all, wm_own.astype(f32), ((1,), (1,)))
    dtemb = dsil * silu_slope(temb_own) + own_cols(per[:, 6] + per[:, 7])
    grad_mod = dot32(low(jax.nn.silu(temb_own)).astype(f32), dmod_all, ((0,), (0,)))
    grad_time2 = dot32(dtemb, sh_all.astype(f32), ((0,), (0,)))
    once = jnp.sum(grad_mod * grad_mod) + jnp.sum(grad_time2 * grad_time2)

    def squares(value):
        return jnp.sum(value * value)

    partial = (
        squares(grad_a)
        + squares(grad_f)
        + squares(grad_y2)
        + squares(grad_y1[:, : text + 1])
    )
    tile = jnp.concatenate(
        [jnp.full((4, 128), partial, f32), jnp.full((4, 128), jnp.sum(loss_t), f32)]
    )
    pad_rows = -(-(n * count) // 8) * 8
    dtembs, vecs, tiles = comm_call(
        functools.partial(middle_kernel, n),
        7,
        (jnp.pad(dtemb, ((0, pad_rows - n * count), (0, 128 - cols))), grad_v, tile),
        [sds((n, pad_rows, 128), f32), sds((4, cols, 128), f32), sds((4, 8, 128), f32)],
        [(n,), (n,), (2, 4), (2, 4), (3,)],
    )
    dtemb_all = dtembs[:, : n * count, :cols].transpose(1, 0, 2).reshape(n * count, width)
    w2_own = lax.dynamic_slice_in_dim(ww[:, 256 : 256 + width], d * cols, cols, 1)
    dsh = dot32(dtemb_all, w2_own.astype(f32), ((1,), (0,)))
    dhid = dsh * silu_slope(own_cols(hid_all))
    grad_time1 = dot32(dhid, feature.astype(f32), ((0,), (0,)))
    extra_rows = jnp.concatenate(
        [
            jnp.sum(dhid, axis=0)[:, None],
            jnp.sum(dtemb, axis=0)[:, None],
            own_cols(jnp.sum(dmod_all, axis=0).reshape(6, width)).T,
        ],
        axis=1,
    )
    grad_v = jnp.sum(vecs, axis=0)
    grad_v = jnp.concatenate([grad_v[:, 0:1], extra_rows, grad_v[:, 9:77]], axis=1)
    partial = jnp.sum(tiles[:, 0, 0]) + once + squares(grad_v) + squares(grad_time1)
    tile = jnp.concatenate(
        [jnp.full((4, 128), partial, f32), jnp.full((4, 128), jnp.sum(tiles[:, 4, 0]), f32)]
    )
    tiles = comm_call(
        functools.partial(dp_gather_kernel, n),
        8,
        (tile,),
        sds((n, 8, 128), f32),
        [(n,), (n,), (1,)],
    )
    grad_norm = jnp.sqrt(jnp.sum(tiles[:, 0, 0]))
    loss_value = jnp.sum(tiles[:, 4, 0])
    factor = jnp.minimum(1.0, max_norm / (grad_norm + 1e-06))

    att_m = jnp.swapaxes(attention_momentum, 1, 2)
    feed_m = jnp.swapaxes(feed_momentum, 1, 2)
    role_m = jnp.where(role == 0, jnp.pad(att_m[0:4], ((0, 4), (0, 0), (0, 0))), att_m[4:12])
    role_f = lax.dynamic_slice_in_dim(feed_m, 2 * role, 2, 0)
    fast = momentum_decay
    look_a = factor * grad_a * (1.0 + fast) + fast * fast * role_m
    look_f = factor * grad_f * (1.0 + fast) + fast * fast * role_f
    ua, uf, ga2, gf2, gy12, gy22 = comm_call(
        functools.partial(collect_kernel, n),
        9,
        (look_a, look_f, grad_a, grad_f, low(grad_y1), grad_y2),
        [
            sds((n, cols, width), f32),
            sds((n, feed_cols, width), f32),
            sds((2, 8, cols, width), f32),
            sds((2, 2, feed_cols, width), f32),
            sds((2, own_rows, text + 128), bf16),
            sds((cols, width), f32),
        ],
        [(8,), (n,), (1,), (7, 3), (7, 3), (7,)],
    )
    xa, xf = local_call(
        muon_kernel,
        [sds((width, width), bf16), sds((hidden, width), bf16)],
        [SM] + [VM] * 2,
        (half_s, ua.reshape(width, width), uf.reshape(hidden, width)),
    )
    xa_all, xf_all = comm_call(
        functools.partial(spread_kernel, n),
        10,
        (xa.reshape(n, cols, width), xf.reshape(n, feed_cols, width)),
        [sds((2, 8, cols, width), bf16), sds((2, 2, feed_cols, width), bf16)],
        [(n,), (8,), (20, 3), (20, 3), (8,)],
    )

    grad_att = jnp.concatenate([ga2[0, 0:4], ga2[1]], axis=0) * factor
    grad_feed = gf2.reshape(4, feed_cols, width) * factor
    full_att = jnp.concatenate([xa_all[0, 0:4], xa_all[1]], axis=0).astype(f32)
    full_feed = xf_all.reshape(4, feed_cols, width).astype(f32)
    att_moment = fast * att_m + grad_att
    feed_moment = fast * feed_m + grad_feed
    shrink = 1.0 - muon_rate * weight_decay
    att_new = att_t * shrink - (muon_rate * 0.2 * math.sqrt(n * cols)) * full_att
    feed_new = feed_t * shrink - (muon_rate * 0.2 * math.sqrt(hidden)) * full_feed

    text_grad = gy12.astype(f32).reshape(2 * own_rows, text + 128)[:cols]
    grad_v = jnp.concatenate(
        [grad_v[:, 0:9], text_grad[:, text : text + 1], grad_v[:, 10:77]], axis=1
    )
    side_grad = jnp.concatenate(
        [
            grad_v[:, 45:61],
            grad_time1,
            grad_time2,
            text_grad[:, :text],
            gy22,
            grad_v[:, 61:77],
            grad_mod,
        ],
        axis=1,
    )
    clock = step_count[0].astype(f32)
    side_new, side_first_new, side_second_new = adamw_update(
        side_t, side_first.T, side_second.T, side_grad * factor, clock
    )
    vector_new, vector_first_new, vector_second_new = adamw_update(
        vector_weights, vector_first, vector_second, grad_v[:, 0:45].T * factor, clock
    )

    def back(value):
        return jnp.swapaxes(value, -1, -2)

    return (
        loss_value,
        grad_norm,
        back(att_new),
        back(att_moment),
        back(feed_new),
        back(feed_moment),
        back(side_new),
        back(side_first_new),
        back(side_second_new),
        vector_new,
        vector_first_new,
        vector_second_new,
        back(low(att_new)),
        back(low(feed_new)),
        back(low(side_new)),
        low(vector_new),
    )


def solution(mesh):
    column = P(None, "dp")
    matrix = P(None, None, "dp")
    return jax.shard_map(
        body,
        mesh=mesh,
        in_specs=(
            P("dp", None, None, None, None),
            P("dp", None, None, None, None),
            P("dp"),
            P("dp", None, None),
            P("dp"),
            matrix,
            matrix,
            column,
            column,
            matrix,
            matrix,
            column,
            column,
            column,
            column,
            P(),
        ),
        out_specs=(
            P(),
            P(),
            matrix,
            matrix,
            matrix,
            matrix,
            column,
            column,
            column,
            column,
            column,
            column,
            matrix,
            matrix,
            column,
            column,
        ),
        check_vma=False,
    )
```

time: 3130 us -> 497 us (0.16)
  waiting for transfers between devices: 1620 us -> 0 us
  matrix products: 505 us -> 7.94 us
  Pallas kernels: 0 us -> 378 us
  other arithmetic: 322 us -> 36.3 us
  starting transfers between devices: 188 us -> 0 us
  local copies, waits for them, and re-layouts: 199 us -> 54.9 us
  loops' own time: 132 us -> 0 us
  blocking collectives: 119 us -> 0 us
    psum x6 -> x0, waiting for transfers between devices: 568 us -> none  [the longest x4 390 us: body(): gram_pair = lax.psum((gram_of(own_attention), gram_of(own_feed)), 'dp')]
    dot_general x270 -> x5, matrix products: 505 us -> 7.94 us  [dot32(): return lax.dot_general(left, right, (dims, ((), ())), precision=highest)]
    reduce_scatter x3 -> x0, waiting for transfers between devices: 490 us -> none  [the longest x1 197 us: body(): lax.psum_scatter(grads[2], 'dp', scatter_dimension=1, tiled=True)]
    pallas_call x0 -> x16, Pallas kernels: none -> 378 us  [the longest x10 306 us: comm_call(): pl.pallas_call(kernel, out_shape=out_shape, in_specs=[ANY] * len(args), o...]
    ppermute x12 -> x0, waiting for transfers between devices: 323 us -> none  [from_behind(): return lax.ppermute(shard, axis, pairs)]
    ppermute x12 -> x0, starting transfers between devices: 186 us -> none  [from_behind(): return lax.ppermute(shard, axis, pairs)]
    all_gather x4 -> x0, waiting for transfers between devices: 177 us -> none  [the longest x1 84.4 us: body(): lax.all_gather(side_weights.astype(jnp.bfloat16), 'dp', axis=1, tiled=True)]
    add x51 -> x5, other arithmetic: 175 us -> 4.97 us  [the longest x1 2.01 us: body(): look_f = factor * grad_f * (1.0 + fast) + fast * fast * role_f]
  transfers between devices with their start and end apart: 26 -> 0, of which waited for: 25 -> 0; matrix products, arithmetic and copies ran while one was open for 8% -> 0% of each run, Pallas kernels for 0% -> 0%
where the time goes in v1:
time: 497 us; the launch traced here: 488 us
  Pallas kernels  378 us (76%)
  local copies, waits for them, and re-layouts  54.9 us (11%)
  other arithmetic  36.3 us (7%)
  between operations  10.7 us (2%)
  matrix products  7.94 us (2%)
    pallas_call x10, Pallas kernels, comm_call(): pl.pallas_call(kernel, out_shape=out_shape, in_specs=[ANY] * len(args), o...  306 us
    pallas_call x6, Pallas kernels, local_call(): pl.pallas_call(kernel, out_shape=out_shape, in_specs=in_specs, out_specs=...  72.5 us

profile of v1, /device:TPU:27, one launch (start us, length us, event | category | flops | bytes accessed | tf_op | source)
XLA Modules:
  0.0 487.9 jit_solution(12120016678429329698)
XLA Ops:
  7.5 1.6 fusion.15.pa
  9.2 1.8 fusion.14.pf
  14.5 40.8 %shard_map.306 = (bf16[4,8,48,384]{3,2,1,0:T(8,128)(2,1)}, bf16[4,8,48,384]{3,2,1,0:T(8,128)(2,1)}, bf16[2,8,192,384]{3,2,1,0:T(8,128)(2,1)}, bf16[8,48,1152]{2,...) custom-call(bf16[4,48,384]{2,1,0:T(8,128)(2,1)} %fusion.15.pa, ...), custom_call_target="tpu_custom_call" | custom-call | tf_op jit(solution)/shard_map/pallas_call | solution.py:644
  59.4 3.1 shard_map.307
  62.4 1.7 slice.216
  66.0 21.9 %shard_map.308.mq = f32[4,8,768]{2,1,0:T(8,128)} custom-call(f32[8,768]{1,0:T(8,128)} %get-tuple-element.84.refs_0_), custom_call_target="tpu_custom_call" | custom-call | tf_op jit(solution)/shard_map/pallas_call | solution.py:644
  89.2 3.4 copy.74
  92.6 3.7 copy.73
  100.4 10.6 %shard_map.309 = (bf16[3,2,64,384]{3,2,1,0:T(8,128)(2,1)}, f32[3,304,192]{2,1,0:T(8,128)}, bf16[3,304,192]{2,1,0:T(8,128)(2,1)}) custom-call(s32[1]{0:T(128)} %bitcast.role, s32[1]{0:T(128)} %bitcast.1.half, bf16[384,128]{1,0:T(8,128)(2,1)} %pad.23.tok, f32[128,384]{1,0:T(8,128)} %constant.139.clone.pos, f32[4,8,768]{2,1,0:T(8,128)} %shard_map.308.mq, ...), custom_call_target="tpu_custom_call" | custom-call | tf_op jit(solution)/shard_map/pallas_call | solution.py:595
  111.7 7.5 %shard_map.310 = (bf16[3,2,64,384]{3,2,1,0:T(8,128)(2,1)}, bf16[2,3,304,192]{3,2,1,0:T(8,128)(2,1)}) custom-call(bf16[3,2,64,384]{3,2,1,0:T(8,128)(2,1)} %get-tuple-element.90.h1s, bf16[3,304,192]{2,1,0:T(8,128)(2,1)} %get-tuple-element.91.gq), custom_call_target="tpu_custom_call" | custom-call | tf_op jit(solution)/shard_map/pallas_call | solution.py:644
  119.2 6.9 %shard_map.311 = (bf16[3,2,64,384]{3,2,1,0:T(8,128)(2,1)}, bf16[10,384,384]{2,1,0:T(8,128)(2,1)}, bf16[2,384,384]{2,1,0:T(8,128)(2,1)}, bf16[2,384,1536]{2,1,0:T...) custom-call(s32[1]{0:T(128)} %bitcast.role, ...), custom_call_target="tpu_custom_call" | custom-call | tf_op jit(solution)/shard_map/pallas_call | solution.py:595
  127.4 43.6 %shard_map.312 = (bf16[3,2,64,384]{3,2,1,0:T(8,128)(2,1)}, f32[2,304,384]{2,1,0:T(8,128)}) custom-call(bf16[3,2,64,384]{3,2,1,0:T(8,128)(2,1)} %get-tuple-element.96.dh1, f32[2,2,304,384]{3,2,1,0:T(8,128)} %get-tuple-element.97.dkv), custom_call_target="tpu_custom_call" | custom-call | tf_op jit(solution)/shard_map/pallas_call | solution.py:644
  171.0 20.1 %shard_map.313 = (bf16[6,384,384]{2,1,0:T(8,128)(2,1)}, bf16[2,384,384]{2,1,0:T(8,128)(2,1)}, bf16[2,384,1536]{2,1,0:T(8,128)(2,1)}, bf16[2,2,304,384]{3,2,1,0:T...) custom-call(s32[1]{0:T(128)} %bitcast.role, s32[1]{0:T(128)} %bitcast.1.half, ...), custom_call_target="tpu_custom_call" | custom-call | tf_op jit(solution)/shard_map/pallas_call | solution.py:595
  191.2 6.0 %shard_map.314 = (bf16[10,384,384]{2,1,0:T(8,128)(2,1)}, bf16[2,384,384]{2,1,0:T(8,128)(2,1)}, bf16[2,384,1536]{2,1,0:T(8,128)(2,1)}, bf16[2,304,384]{2,1,0:T(8,...) custom-call(bf16[6,384,384]{2,1,0:T(8,128)(2,1)} %get-tuple-element.102.acts_s, ...), custom_call_target="tpu_custom_call" | custom-call | tf_op jit(solution)/shard_map/pallas_call | solution.py:644
  197.2 11.8 %shard_map.315 = (bf16[8,384,384]{2,1,0:T(8,128)(2,1)}, bf16[2,1536,384]{2,1,0:T(8,128)(2,1)}, f32[384,384]{1,0:T(8,128)}, bf16[192,4224]{1,0:T(8,128)(2,1)}) custom-call(s32[1]{0:T(128)} %bitcast.role, s32[1]{0:T(128)} %bitcast.1.half, bf16[6,384,384]{2,1,0:T(8,128)(2,1)} %get-tuple-element.102.acts_s, bf16[10,384,384]{2,1,0:T(8,128)(2,1)} %get-tuple-element.103.acts_t, ...), custom_call_target="tpu_custom_call" | custom-call | tf_op jit(solution)/shard_map/pallas_call | solution.py:595
  209.6 52.2 %shard_map.316 = (bf16[8,8,48,384]{3,2,1,0:T(8,128)(2,1)}, bf16[8,2,192,384]{3,2,1,0:T(8,128)(2,1)}, f32[8,48,384]{2,1,0:T(8,128)}, bf16[8,24,4224]{2,1,0:T(8,12...) custom-call(bf16[8,8,48,384]{3,2,1,0:T(8,128)(2,1)} %bitcast.161, bf16[2,8,192,384]{3,2,1,0:T(8,128)(2,1)} %bitcast.162, ...), custom_call_target="tpu_custom_call" | custom-call | tf_op jit(solution)/shard_map/pallas_call | solution.py:644
  261.8 1.6 reduce_sum.208.vec
  272.9 1.8 multiply_reduce_fusion.2
  284.4 67.8 %shard_map.317 = (f32[8,24,128]{2,1,0:T(8,128)}, f32[4,48,128]{2,1,0:T(8,128)}, f32[4,8,128]{2,1,0:T(8,128)}) custom-call(f32[24,128]{1,0:T(8,128)} %pad.26.dtemb, f32[48,128]{1,0:T(8,128)} %reduce_sum.208.vec, f32[8,128]{1,0:T(8,128)} %concatenate.40.tile), custom_call_target="tpu_custom_call" | custom-call | tf_op jit(solution)/shard_map/pallas_call | solution.py:644
  358.8 1.6 reshape.209
  365.8 2.2 multiply_reduce_fusion.5
  369.9 5.9 %shard_map.318 = f32[8,8,128]{2,1,0:T(8,128)} custom-call(f32[8,128]{1,0:T(8,128)} %concatenate.43.src), custom_call_target="tpu_custom_call" | custom-call | tf_op jit(solution)/shard_map/pallas_call | solution.py:644
  378.1 2.0 bitcast_add_fusion.2.uf
  380.1 1.7 fusion.7.ua
  381.7 25.4 %shard_map.319 = (f32[8,48,384]{2,1,0:T(8,128)}, f32[8,192,384]{2,1,0:T(8,128)}, f32[2,8,48,384]{3,2,1,0:T(8,128)}, f32[2,2,192,384]{3,2,1,0:T(8,128)}, bf16[2,24,4224]{2,1,0:T(8,128)(2,1)}, /*index=5*/f32[48,384]{1,0:T(8,128)}) custom-call(f32[8,48,384]{2,1,0:T(8,128)} %fusion.7.ua, f32[2,192,384]{2,1,0:T(8,128)} %bitcast_add_fusion.2.uf, ...), custom_call_target="tpu_custom_call" | custom-call | tf_op jit(solution)/shard_map/pallas_call | solution.py:644
  407.2 20.0 %shard_map.320 = (bf16[384,384]{1,0:T(8,128)(2,1)}, bf16[1536,384]{1,0:T(8,128)(2,1)}) custom-call(s32[1]{0:T(128)} %bitcast.1.half, f32[384,384]{1,0:T(8,128)} %bitcast.181, f32[1536,384]{1,0:T(8,128)} %bitcast.163), custom_call_target="tpu_custom_call" | custom-call | tf_op jit(solution)/shard_map/pallas_call | solution.py:595
  427.2 34.4 %shard_map.321 = (bf16[2,8,48,384]{3,2,1,0:T(8,128)(2,1)}, bf16[2,2,192,384]{3,2,1,0:T(8,128)(2,1)}) custom-call(bf16[8,48,384]{2,1,0:T(8,128)(2,1)} %bitcast.184, bf16[8,192,384]{2,1,0:T(8,128)(2,1)} %bitcast.174), custom_call_target="tpu_custom_call" | custom-call | tf_op jit(solution)/shard_map/pallas_call | solution.py:644
  461.7 1.6 slice_bitcast_fusion.3
  463.3 1.7 slice_bitcast_fusion.2
  470.2 2.0 concatenate.46
  479.8 3.3 fusion.10
  483.1 3.5 convert_bitcast_fusion
  (155 shorter events, 64.0 us)
Async XLA Ops:
  0.6 10.3 %copy-start.4 = (f32[12,384,48]{1,2,0:T(8,128)S(1)}, f32[12,384,48]{1,2,0:T(8,128)}, u32[]{:S(2)}) copy-start(f32[12,384,48]{1,2,0:T(8,128)} %param.24) | copy-start | bytes 2654212
  0.7 11.0 %copy-start = (f32[7456,48]{0,1:T(8,128)S(1)}, f32[7456,48]{0,1:T(8,128)}, u32[]{:S(2)}) copy-start(f32[7456,48]{0,1:T(8,128)} %param.26) | copy-start | bytes 4294660
  4.7 7.1 %copy-start.21 = (f32[45,48]{0,1:T(8,128)}, f32[45,48]{0,1:T(8,128)S(1)}, u32[]{:S(2)}) copy-start(f32[45,48]{0,1:T(8,128)S(1)} %copy.77) | copy-start | bytes 25924
  11.8 43.5 %copy-start.5 = (bf16[48,7456]{1,0:T(8,128)(2,1)}, bf16[48,7456]{1,0:T(8,128)(2,1)S(1)}, u32[]{:S(2)}) copy-start(bf16[48,7456]{1,0:T(8,128)(2,1)S(1)} %bitcast_convert_fusion) | copy-start | bytes 2147332
  59.4 28.5 %copy-start.16 = (f32[3,4,4,16,16]{4,3,2,1,0:T(8,128)S(1)}, f32[3,4,4,16,16]{4,3,2,1,0:T(8,128)}, u32[]{:S(2)}) copy-start(f32[3,4,4,16,16]{4,3,2,1,0:T(8,128)} %param.20) | copy-start | bytes 147460
  59.4 28.5 %copy-start.17 = (f32[3,4,4,16,16]{4,3,2,1,0:T(8,128)S(1)}, f32[3,4,4,16,16]{4,3,2,1,0:T(8,128)}, u32[]{:S(2)}) copy-start(f32[3,4,4,16,16]{4,3,2,1,0:T(8,128)} %param.19) | copy-start | bytes 147460
  65.1 206.4 %copy-start.28 = (f32[24,384]{1,0:T(8,128)}, f32[24,384]{1,0:T(8,128)S(1)}, u32[]{:S(2)}) copy-start(f32[24,384]{1,0:T(8,128)S(1)} %reshape.208) | copy-start | bytes 110596
  197.2 11.8 %copy-start.23 = (f32[4,3,8,384]{3,2,1,0:T(8,128)S(1)}, f32[4,3,8,384]{3,2,1,0:T(8,128)}, u32[]{:S(2)}) copy-start(f32[4,3,8,384]{3,2,1,0:T(8,128)} %get-tuple-element.123) | copy-start | bytes 442372
  264.5 11.5 %copy-start.10 = (bf16[8,24,4224]{2,1,0:T(8,128)(2,1)S(1)}, bf16[8,24,4224]{2,1,0:T(8,128)(2,1)}, u32[]{:S(2)}) copy-start(bf16[8,24,4224]{2,1,0:T(8,128)(2,1)} %get-tuple-element.130) | copy-start | bytes 4866052
  276.0 1.7 copy-start.8
  277.8 1.7 copy-start.7
  278.9 101.1 %copy-start.2 = (f32[8,48,384]{2,1,0:T(8,128)}, f32[8,48,384]{2,1,0:T(8,128)S(1)}, u32[]{:S(2)}) copy-start(f32[8,48,384]{2,1,0:T(8,128)S(1)} %get-tuple-element.213.ga) | copy-start | bytes 1769476
  280.5 99.6 %copy-start.1 = (f32[2,192,384]{2,1,0:T(8,128)}, f32[2,192,384]{2,1,0:T(8,128)S(1)}, u32[]{:S(2)}) copy-start(f32[2,192,384]{2,1,0:T(8,128)S(1)} %get-tuple-element.211.gf) | copy-start | bytes 1769476
  356.6 23.5 %copy-start.3 = (f32[12,384,48]{1,2,0:T(8,128)S(1)}, f32[12,384,48]{1,2,0:T(8,128)}, u32[]{:S(2)}) copy-start(f32[12,384,48]{1,2,0:T(8,128)} %param.28) | copy-start | bytes 2654212
  427.2 37.8 %copy-start.13 = (f32[2,8,48,384]{3,2,1,0:T(8,128)S(1)}, f32[2,8,48,384]{3,2,1,0:T(8,128)}, u32[]{:S(2)}) copy-start(f32[2,8,48,384]{3,2,1,0:T(8,128)} %get-tuple-element.141) | copy-start | bytes 3538948
  461.7 4.1 copy-start.14
  465.7 1.3 copy-start.9
  467.0 1.4 copy-start.15
  467.0 1.5 copy-start.18
  467.0 1.5 copy-start.19
  467.0 1.5 copy-start.20
  467.0 1.5 copy-start.25
  470.2 2.0 copy-start.22
  470.2 2.0 copy-start.24
  472.2 2.9 copy-start.6
  475.1 3.3 copy-start.27
  475.1 4.0 copy-start.26
  479.8 3.3 copy-start.11
  479.8 3.3 copy-start.12
